TPU v7x, 128 devices: a whole 4x4x4 slice. The times are simulated.
128 devices in a mesh: lat: 8 (over y_lo, z), lon: 16 (over x, y_hi, core).
Axes of the slice: x: 4, y: 4 (y_hi: 2, y_lo: 2; y = y_hi * 2 + y_lo), z: 4, core: 2. Of those that a mesh axis runs over, the one named last changes fastest.
Arguments:
- state: bfloat16 [64, 6144, 128], P('lat', 'lon'), may hold values from -6 to 6
- forcing: bfloat16 [64, 6144, 128], P('lat', 'lon'), may hold values from -4 to 4
- cotangent: bfloat16 [64, 6144, 128], P('lat', 'lon'), may hold values from -6 to 6
- land_mask: int32 [64, 6144], P('lat', 'lon'), may hold values 0 or 1
- dw_weight: bfloat16 [7, 7, 128], replicated, may hold values from -0.875 to 0.875
- dw_bias: float32 [128], replicated, may hold values from -3 to 3
- norm_gain: float32 [128], replicated, may hold values from 0.5 to 1.5
- norm_bias: float32 [128], replicated, may hold values from -3 to 3
- up_weight: bfloat16 [128, 512], replicated, may hold values from -0.5 to 0.5
- up_bias: float32 [512], replicated, may hold values from -3 to 3
- down_weight: bfloat16 [512, 128], replicated, may hold values from -0.25 to 0.25
- down_bias: float32 [128], replicated, may hold values from -3 to 3
- layer_scale: float32 [128], replicated, may hold values from 0.3 to 1
- owner: int32 [786432, 1], P(('lat', 'lon')), may hold values from 0 to 127; in each aligned block of 6144 rows (0 to 6143, 6144 to 12287, ...) at most 96 rows name the same one
- atmos_cell: int32 [786432], P(('lat', 'lon')), may hold values from 0 to 511
- weight_index: int32 [786432], P(('lat', 'lon')), may hold values from 0 to 15
- intersection_weights: float32 [16], replicated, may hold values from 0.1 to 1
Outputs:
- result: bfloat16 [64, 6144, 128], P('lat', 'lon')
- grad_dw: float32 [7, 7, 128], replicated
- grad_up: float32 [128, 512], replicated
- grad_down: float32 [512, 128], replicated
- forcing_grad: float32 [65536, 128], P(('lat', 'lon'))
Inputs may be any that keep to these rules, and one draw needn't show every extreme that they name: At most 96 entries of one device name the same owner, and in every draw some device's entries name some owner exactly 96 times.
All inputs are finite; a program needn't handle non-finite values. No bound on the sum of `land_mask` on one device may be relied on, other than what follows from the above.
Results may differ from a plain program's by a relative error of at most 0.0071.
Values may be sent and summed in bfloat16 or wider, within the bound.
A program may use at most 128 MiB of HBM per device.

v0:
```python
import jax
import jax.numpy as jnp
from jax import lax
from jax.sharding import PartitionSpec as P

A_DEV = 512


gelu_scale = 0.7978845608028654
cubic_coef = 0.044715


def extended(block, sides, width, periodic):
    for axis, dim in sides:
        count = lax.axis_size(axis)
        forward = [(i, i + 1) for i in range(count - 1)]
        if periodic:
            forward.append((count - 1, 0))
        backward = [(target, source) for source, target in forward]
        low = lax.ppermute(
            lax.slice_in_dim(block, block.shape[dim] - width, None, axis=dim), axis, forward
        )
        high = lax.ppermute(lax.slice_in_dim(block, 0, width, axis=dim), axis, backward)
        block = jnp.concatenate([low, block, high], axis=dim)
    return block


def partner_2(array, axis, distance):
    return lax.ppermute(array, axis, [(i, i ^ 1 << distance) for i in range(lax.axis_size(axis))])


def gelu_pair(pre):
    inner = gelu_scale * (pre + cubic_coef * pre * pre * pre)
    tanh_value = jnp.tanh(inner)
    value = 0.5 * pre * (1.0 + tanh_value)
    slope = 0.5 * (1.0 + tanh_value) + 0.5 * pre * (1.0 - tanh_value * tanh_value) * gelu_scale * (
        1.0 + 3.0 * cubic_coef * pre * pre
    )
    return (value, slope)


def depthwise(padded, kernel):
    channels = padded.shape[-1]
    convolved = lax.conv_general_dilated(
        padded[None],
        kernel[:, :, None, :],
        (1, 1),
        "VALID",
        dimension_numbers=("NHWC", "HWIO", "NHWC"),
        feature_group_count=channels,
        preferred_element_type=jnp.float32,
    )
    return convolved[0]


def block_pass(
    padded,
    state,
    forcing,
    cotangent,
    land,
    dw_weight,
    dw_bias,
    norm_gain,
    norm_bias,
    up_weight,
    up_bias,
    down_weight,
    down_bias,
    layer_scale,
):
    tile_rows, tile_cols, channels = state.shape
    conv = depthwise(padded, dw_weight) + dw_bias
    average = jnp.mean(conv, axis=-1, keepdims=True)
    centred = conv - average
    variance = jnp.mean(centred * centred, axis=-1, keepdims=True)
    inv_std = lax.rsqrt(variance + 1e-06)
    normed = centred * inv_std
    mixed = (normed * norm_gain + norm_bias + forcing.astype(jnp.float32)).astype(jnp.bfloat16)
    flat = mixed.reshape(-1, channels)
    pre = jnp.dot(flat, up_weight, preferred_element_type=jnp.float32) + up_bias
    activated, slope = gelu_pair(pre)
    hidden = activated.astype(jnp.bfloat16)
    projected = jnp.dot(hidden, down_weight, preferred_element_type=jnp.float32) + down_bias
    ocean = land.astype(jnp.float32).reshape(-1, 1)
    result = (
        ocean * (state.reshape(-1, channels).astype(jnp.float32) + layer_scale * projected)
    ).astype(jnp.bfloat16)
    grad_out = (ocean * layer_scale * cotangent.reshape(-1, channels).astype(jnp.float32)).astype(
        jnp.bfloat16
    )
    down_term = jnp.dot(hidden.T, grad_out, preferred_element_type=jnp.float32)
    grad_hidden = jnp.dot(grad_out, down_weight.T, preferred_element_type=jnp.float32)
    grad_pre = (grad_hidden * slope).astype(jnp.bfloat16)
    up_term = jnp.dot(flat.T, grad_pre, preferred_element_type=jnp.float32)
    grad_mixed = jnp.dot(grad_pre, up_weight.T, preferred_element_type=jnp.float32).reshape(
        tile_rows, tile_cols, channels
    )
    gained = grad_mixed * norm_gain
    grad_conv = (
        inv_std
        * (
            gained
            - jnp.mean(gained, axis=-1, keepdims=True)
            - normed * jnp.mean(gained * normed, axis=-1, keepdims=True)
        )
    ).astype(jnp.bfloat16)
    conv_term = depthwise(padded, grad_conv)
    return (
        result.reshape(tile_rows, tile_cols, channels),
        grad_mixed,
        conv_term,
        up_term,
        down_term,
    )


def on_device(
    state,
    forcing,
    cotangent,
    land_mask,
    dw_weight,
    dw_bias,
    norm_gain,
    norm_bias,
    up_weight,
    up_bias,
    down_weight,
    down_bias,
    layer_scale,
    owner,
    atmos_cell,
    weight_index,
    intersection_weights,
):
    margin = dw_weight.shape[0] // 2
    tile_rows, tile_cols, channels = state.shape
    lat_count = lax.axis_size("lat")
    lon_count = lax.axis_size("lon")
    lon_ext = extended(state, (("lon", 1),), margin, True)
    padded = extended(lon_ext, (("lat", 0),), margin, False)
    north_rim = lon_ext[tile_rows - margin :]
    bit_total = lon_count.bit_length() - 1
    partner = north_rim
    for bit_number in range(bit_total):
        partner = partner_2(partner, "lon", bit_number)
    mirrored = partner[::-1, ::-1]
    northmost = lax.axis_index("lat") == lat_count - 1
    north_rows = jnp.where(northmost, mirrored, padded[tile_rows + margin :])
    padded = jnp.concatenate([padded[: tile_rows + margin], north_rows], axis=0)
    result, grad_mixed, conv_term, up_term, down_term = block_pass(
        padded,
        state,
        forcing,
        cotangent,
        land_mask,
        dw_weight,
        dw_bias,
        norm_gain,
        norm_bias,
        up_weight,
        up_bias,
        down_weight,
        down_bias,
        layer_scale,
    )
    conv_sum, up_sum, down_sum = lax.psum((conv_term, up_term, down_term), ("lat", "lon"))
    scale = float(tile_rows * lat_count * tile_cols * lon_count) ** (-0.5)
    grad_dw = conv_sum * scale
    grad_up = up_sum * scale
    grad_down = down_sum * scale
    entries = owner.shape[0]
    devices = lat_count * lon_count
    capacity = max(2, 2 * entries // devices)
    table_hit = (
        weight_index[:, None] == jnp.arange(intersection_weights.shape[0], dtype=jnp.int32)[None, :]
    )
    entry_weights = jnp.sum(jnp.where(table_hit, intersection_weights[None, :], 0.0), axis=1)
    per_entry = jnp.repeat(
        grad_mixed.reshape(tile_rows * tile_cols, channels),
        entries // (tile_rows * tile_cols),
        axis=0,
    )
    values = (entry_weights[:, None] * per_entry).astype(jnp.bfloat16)
    dest_owner = owner[:, 0]
    sorting = jnp.argsort(dest_owner, stable=True)
    sorted_owner = dest_owner[sorting]
    owner_ids = jnp.arange(devices, dtype=jnp.int32)
    owner_load = jnp.sum((dest_owner[:, None] == owner_ids[None, :]).astype(jnp.int32), axis=0)
    owner_start = jnp.cumsum(owner_load) - owner_load
    first_slot = jnp.sum(
        jnp.where(sorted_owner[:, None] == owner_ids[None, :], owner_start[None, :], 0), axis=1
    )
    slot_rank = jnp.arange(entries, dtype=jnp.int32) - first_slot
    slot_index = sorted_owner * capacity + slot_rank
    send_rows = (
        jnp.zeros((devices * capacity, channels), jnp.bfloat16).at[slot_index].set(values[sorting])
    )
    send_cells = jnp.zeros((devices * capacity,), jnp.int32).at[slot_index].set(atmos_cell[sorting])
    recv_rows, recv_cells = (
        lax.all_to_all(
            send_rows.reshape(devices, capacity, channels),
            ("lat", "lon"),
            split_axis=0,
            concat_axis=0,
            tiled=True,
        ),
        lax.all_to_all(
            send_cells.reshape(devices, capacity),
            ("lat", "lon"),
            split_axis=0,
            concat_axis=0,
            tiled=True,
        ),
    )
    forcing_grad = jax.ops.segment_sum(
        recv_rows.reshape(-1, channels).astype(jnp.float32),
        recv_cells.reshape(-1),
        num_segments=A_DEV,
    )
    return (result, grad_dw, grad_up, grad_down, forcing_grad)


def solution(mesh):
    in_specs = (
        P("lat", "lon", None),
        P("lat", "lon", None),
        P("lat", "lon", None),
        P("lat", "lon"),
        P(),
        P(),
        P(),
        P(),
        P(),
        P(),
        P(),
        P(),
        P(),
        P(("lat", "lon"), None),
        P(("lat", "lon")),
        P(("lat", "lon")),
        P(),
    )
    out_specs = (P("lat", "lon", None), P(), P(), P(), P(("lat", "lon"), None))
    return jax.shard_map(
        on_device, mesh=mesh, in_specs=in_specs, out_specs=out_specs, check_vma=False
    )
```

profile of v0, /device:TPU:1, one launch (start us, length us, event | category | flops | bytes accessed | tf_op | source)
XLA Modules:
  0.0 523.5 jit_solution(2055664326596326524)
XLA Ops:
  8.0 4.4 collective-permute-start
  12.3 7.4 %sort.17 = (s32[6144]{0:T(1024)}, s32[6144]{0:T(1024)S(1)}) sort(s32[6144]{0:T(1024)} %bitcast.82, s32[6144]{0:T(1024)S(1)} %iota.16), dimensions={0}, to_apply=%region_7.8 | sort | flops 79872 | bytes 98304 | tf_op jit(solution)/shard_map/jit(argsort)/sort | solution.py:187
  21.0 2.5 collective-permute-start.3
  23.6 34.3 %gather_fusion = s32[6144]{0:T(1024)S(1)} fusion(s32[6144]{0:T(1024)S(1)} %bitcast.83, s32[6144]{0:T(1024)S(1)} %fusion.47), kind=kCustom, calls=%fused_computation | custom fusion | bytes 73728 | tf_op jit(solution)/shard_map/gather | solution.py:188
  57.9 2.7 convert_reduce_fusion
  62.0 3.7 select_reduce_fusion
  65.7 5.6 %collective-permute-done.4 = bf16[3,390,128]{2,1,0:T(8,128)(2,1)S(1)} collective-permute-done((bf16[3,390,128]{2,1,0:T(8,128)(2,1)S(1)}, bf16[3,390,128]{2,1,0:T(8,128)(2,1)S(1)}, u32[]{:S(2)}, u32[]{:S(2)}) %collective-permute-start.4) | collective-permute-done | bytes 299552 | tf_op jit(solution)/shard_map/ppermute | solution.py:29
  71.5 34.3 %gather_fusion.1 = s32[6144]{0:T(1024)S(1)} fusion(s32[6144]{0:T(1024)S(1)} %copy-done.2, s32[6144]{0:T(1024)S(1)} %fusion.47), kind=kCustom, calls=%fused_computation.1 | custom fusion | bytes 73728 | tf_op jit(solution)/shard_map/gather | solution.py:200
  105.8 23.0 %scatter_custom_fusion = s32[12288]{0:T(1024)S(1)} fusion(s32[6144]{0:T(1024)S(1)} %bitcast.99, s32[6144]{0:T(1024)S(1)} %gather_fusion.1, s32[]{:T(128)} %constant.47.clone.1), kind=kCustom, calls=%fused_computation.83 | custom fusion | bytes 49156 | tf_op jit(solution)/shard_map/scatter | solution.py:200
  129.6 10.0 %all-to-all-start = ((s32[128,1,96]{2,1,0:T(1,128)}), s32[128,1,96]{2,1,0:T(1,128)S(1)}, u32[]{:S(2)}, u32[]{:S(2)}) async-start(s32[128,1,96]{2,1,0:T(1,128)} %bitcast.18), calls=%async_computation | async-start | bytes 131072 | tf_op jit(solution)/shard_map/all_to_all | solution.py:209
  141.0 2.9 collective-permute-start.6
  145.3 4.0 collective-permute-start.2
  157.6 5.5 %fusion.41 = f32[8,8,49,128]{3,1,2,0:T(8,128)S(1)} fusion(bf16[14,1,7,6,128]{4,2,3,0,1:T(8,128)(2,1)S(1)} %slice.25, bf16[14,1,8,49,128]{4,2,3,0,1:T(8,128)(2,1)S(1)} %copy.69, pred[8,49]{0,1:T(8,128)(4,1)S(1)} %copy-done.31, bf16[7,7,1,128]{3,1,0,2:T(8,128)(2,1)S(1)} %bitcast.102), kind=kOutput, calls=%fused_computation.65 | convolution fusion | flops 44470272 | bytes 3174024 | tf_op jit(solution)/shard_map/conv_general_dilated | solution.py:44
  169.8 3.2 add_convert_fusion
  177.8 3.7 multiply_convert_fusion
  181.5 4.7 fusion.6
  192.9 55.3 %scatter_custom_fusion.1 = bf16[12288,128]{1,0:T(8,128)(2,1)} fusion(s32[6144]{0:T(1024)} %bitcast.100, bf16[6144,128]{1,0:T(8,128)(2,1)} %multiply_convert_fusion.1, s32[6144]{0:T(1024)S(1)} %fusion.47, bf16[]{:T(256)} %constant.51.clone.1), kind=kCustom, calls=%fused_computation.56 | custom fusion | bytes 3146240 | tf_op jit(solution)/shard_map/scatter | solution.py:198
  248.3 12.7 %all-to-all-start.1 = ((bf16[128,96,128]{2,1,0:T(8,128)(2,1)}), bf16[128,96,128]{2,1,0:T(8,128)(2,1)}, u32[]{:S(2)}, u32[]{:S(2)}) async-start(bf16[128,96,128]{2,1,0:T(8,128)(2,1)} %bitcast.91), calls=%async_computation.1 | async-start | bytes 6291456 | tf_op jit(solution)/shard_map/all_to_all | solution.py:202
  261.0 3.8 fusion.57
  266.5 5.9 %fusion.33 = bf16[8,384,1,128]{3,0,1,2:T(8,128)(2,1)S(1)} fusion(f32[8,384,1,128]{3,1,0,2:T(8,128)S(1)} %bitcast.90, f32[8,384]{0,1:T(8,128)} %copy.79, f32[8,384]{0,1:T(8,128)S(1)} %broadcast_multiply_fusion.2, f32[128]{0:T(128)} %param.22, f32[8,384]{0,1:T(8,128)} %copy.75, f32[128]{0:T(128)} %param.23, f32[8,384]{0,1:T(8,128)} %add_rsqrt_fusion, ...), kind=kLoop, calls=%fused_computation.51 | loop fusion | flops 3538944 | bytes 3982336 | tf_op jit(solution)/shard_map/convert_element_type | solution.py:107
  272.5 20.4 %fusion.14 = f32[1,7,7,128]{3,0,2,1:T(1,128)S(1)} fusion(bf16[1,14,390,128]{3,2,1,0:T(8,128)(2,1)S(1)} %copy-done.8, bf16[8,384,1,128]{3,0,1,2:T(8,128)(2,1)S(1)} %fusion.33), kind=kOutput, calls=%fused_computation.30 | convolution fusion | flops 38535168 | bytes 2209280 | tf_op jit(solution)/shard_map/conv_general_dilated | solution.py:44
  294.8 68.0 %psum.21 = f32[7,7,128]{2,1,0:T(8,128)S(1)} all-reduce(f32[7,7,128]{2,1,0:T(8,128)S(1)} %bitcast.96), channel_id=1, replica_groups=mesh['lat'=8,'lon'=16] {'lat','lon'}, use_global_device_ids=true, to_apply=%region_4.5 | all-reduce | flops 6272 | bytes 50176 | tf_op jit(solution)/shard_map/psum | solution.py:168
  363.4 71.4 %all-reduce.3.cloned.1.call-done = (f32[128,512]{1,0:T(8,128)}, f32[512,128]{1,0:T(8,128)}) async-done(((f32[128,512]{1,0:T(8,128)}, f32[512,128]{1,0:T(8,128)}), (f32[128,512]{1,0:T(8,128)}, f32[512,128]{1,0:T(8,128)})) %all-reduce.3.cloned.1.call-update) | async-done | bytes 524304 | tf_op jit(solution)/shard_map/psum | solution.py:168
  438.2 78.0 %scatter_custom_fusion.2 = f32[512,128]{1,0:T(8,128)} fusion(s32[12288]{0:T(1024)} %reshape.267, bf16[12288,128]{1,0:T(8,128)(2,1)} %bitcast.24, f32[]{:T(128)} %constant.20.clone.1), kind=kCustom, calls=%fused_computation.15 | custom fusion | flops 3145728 | bytes 3408384 | tf_op jit(solution)/shard_map/scatter-add | solution.py:217
  (130 shorter events, 41.1 us)
Async XLA Ops:
  7.2 169.8 %copy-start = (bf16[128,512]{1,0:T(8,128)(2,1)S(1)}, bf16[128,512]{1,0:T(8,128)(2,1)}, u32[]{:S(2)}) copy-start(bf16[128,512]{1,0:T(8,128)(2,1)} %param.25) | copy-start | bytes 393220
  8.0 11.8 %collective-permute-start = (bf16[8,3,128]{2,1,0:T(4,128)(2,1)S(1)}, bf16[8,3,128]{2,1,0:T(4,128)(2,1)S(1)}, u32[]{:S(2)}, u32[]{:S(2)}) collective-permute-start(bf16[8,3,128]{2,1,0:T(4,128)(2,1)S(1)} %get-tuple-element.15), channel_id=1, source_target_pairs={{0,1},{1,2},{2,3},{3,4},{4,5},{5,6},{6,7},{7,8},{8,9},{9,10},{10,1... | collective-permute-start | bytes 18440 | tf_op jit(solution)/shard_map/ppermute | solution.py:20
  12.3 7.5 %collective-permute-start.1 = (bf16[8,3,128]{2,1,0:T(4,128)(2,1)S(1)}, bf16[8,3,128]{2,1,0:T(4,128)(2,1)S(1)}, u32[]{:S(2)}, u32[]{:S(2)}) collective-permute-start(bf16[8,3,128]{2,1,0:T(4,128)(2,1)S(1)} %get-tuple-element.16), channel_id=1, source_target_pairs={{1,0},{2,1},{3,2},{4,3},{5,4},{6,5},{7,6},{8,7},{9,8},{10,9},{11,1... | collective-permute-start | bytes 18440 | tf_op jit(solution)/shard_map/ppermute | solution.py:23
  21.0 40.0 %collective-permute-start.3 = (bf16[3,390,128]{2,1,0:T(8,128)(2,1)S(1)}, bf16[3,390,128]{2,1,0:T(8,128)(2,1)S(1)}, u32[]{:S(2)}, u32[]{:S(2)}) collective-permute-start(bf16[3,390,128]{2,1,0:T(8,128)(2,1)S(1)} %get-tuple-element.14), channel_id=1, source_target_pairs={{0,1},{1,0},{2,3},{3,2},{4,5},{5,4},{6,7},{7,6},{8,9},{9,8},{10,11... | collective-permute-start | bytes 898568 | tf_op jit(solution)/shard_map/ppermute | solution.py:29
  61.0 10.3 %collective-permute-start.4 = (bf16[3,390,128]{2,1,0:T(8,128)(2,1)S(1)}, bf16[3,390,128]{2,1,0:T(8,128)(2,1)S(1)}, u32[]{:S(2)}, u32[]{:S(2)}) collective-permute-start(bf16[3,390,128]{2,1,0:T(8,128)(2,1)S(1)} %collective-permute-done.3), channel_id=1, source_target_pairs={{0,2},{1,3},{2,0},{3,1},{4,6},{5,7},{6,4},{7,5},{8,10},{9,11},{10,... | collective-permute-start | bytes 898568 | tf_op jit(solution)/shard_map/ppermute | solution.py:29
  71.3 69.7 %collective-permute-start.5 = (bf16[3,390,128]{2,1,0:T(8,128)(2,1)S(1)}, bf16[3,390,128]{2,1,0:T(8,128)(2,1)S(1)}, u32[]{:S(2)}, u32[]{:S(2)}) collective-permute-start(bf16[3,390,128]{2,1,0:T(8,128)(2,1)S(1)} %collective-permute-done.4), channel_id=1, source_target_pairs={{0,4},{1,5},{2,6},{3,7},{4,0},{5,1},{6,2},{7,3},{8,12},{9,13},{10,... | collective-permute-start | bytes 898568 | tf_op jit(solution)/shard_map/ppermute | solution.py:29
  71.5 34.4 %copy-start.18 = (s32[6144,1]{0,1:T(1,128)}, s32[6144,1]{0,1:T(1,128)S(1)}, u32[]{:S(2)}) copy-start(s32[6144,1]{0,1:T(1,128)S(1)} %compare_select_fusion) | copy-start | bytes 73732
  71.5 68.1 %copy-start.21 = (s32[8,384]{1,0:T(8,128)S(1)}, s32[8,384]{1,0:T(8,128)}, u32[]{:S(2)}) copy-start(s32[8,384]{1,0:T(8,128)} %param.20) | copy-start | bytes 36868
  71.5 72.5 %copy-start.10 = (bf16[8,384,128]{2,1,0:T(8,128)(2,1)S(1)}, bf16[8,384,128]{2,1,0:T(8,128)(2,1)}, u32[]{:S(2)}) copy-start(bf16[8,384,128]{2,1,0:T(8,128)(2,1)} %param.19) | copy-start | bytes 2359300
  71.5 72.5 %copy-start.24 = (f32[128]{0:T(128)S(1)}, f32[128]{0:T(128)}, u32[]{:S(2)}) copy-start(f32[128]{0:T(128)} %param.29) | copy-start | bytes 1540
  105.8 43.5 %copy-start.17 = (s32[6144]{0:T(1024)S(1)}, s32[6144]{0:T(1024)}, u32[]{:S(2)}) copy-start(s32[6144]{0:T(1024)} %param.32) | copy-start | bytes 73732
  105.8 43.5 %copy-start.23 = (f32[16]{0:T(128)S(1)}, f32[16]{0:T(128)}, u32[]{:S(2)}) copy-start(f32[16]{0:T(128)} %param.33) | copy-start | bytes 196
  129.6 20.0 %all-to-all-start = ((s32[128,1,96]{2,1,0:T(1,128)}), s32[128,1,96]{2,1,0:T(1,128)S(1)}, u32[]{:S(2)}, u32[]{:S(2)}) async-start(s32[128,1,96]{2,1,0:T(1,128)} %bitcast.18), calls=%async_computation | async-start | bytes 131072 | tf_op jit(solution)/shard_map/all_to_all | solution.py:209
  139.6 13.2 %collective-permute-start.7 = (bf16[3,390,128]{2,1,0:T(8,128)(2,1)S(1)}, bf16[3,390,128]{2,1,0:T(8,128)(2,1)S(1)}, u32[]{:S(2)}, u32[]{:S(2)}) collective-permute-start(bf16[3,390,128]{2,1,0:T(8,128)(2,1)S(1)} %get-tuple-element.13), channel_id=1, source_target_pairs={{16,0},{32,16},{48,32},{64,48},{80,64},{96,80},{112,96},{17,1},{33... | collective-permute-start | bytes 898568 | tf_op jit(solution)/shard_map/ppermute | solution.py:23
  141.0 10.5 %collective-permute-start.6 = (bf16[3,390,128]{2,1,0:T(8,128)(2,1)S(1)}, bf16[3,390,128]{2,1,0:T(8,128)(2,1)S(1)}, u32[]{:S(2)}, u32[]{:S(2)}) collective-permute-start(bf16[3,390,128]{2,1,0:T(8,128)(2,1)S(1)} %collective-permute-done.5), channel_id=1, source_target_pairs={{0,8},{1,9},{2,10},{3,11},{4,12},{5,13},{6,14},{7,15},{8,0},{9,1},... | collective-permute-start | bytes 898568 | tf_op jit(solution)/shard_map/ppermute | solution.py:29
  145.3 9.5 %collective-permute-start.2 = (bf16[3,390,128]{2,1,0:T(8,128)(2,1)S(1)}, bf16[3,390,128]{2,1,0:T(8,128)(2,1)S(1)}, u32[]{:S(2)}, u32[]{:S(2)}) collective-permute-start(bf16[3,390,128]{2,1,0:T(8,128)(2,1)S(1)} %get-tuple-element.14), channel_id=1, source_target_pairs={{0,16},{16,32},{32,48},{48,64},{64,80},{80,96},{96,112},{1,17},{17... | collective-permute-start | bytes 898568 | tf_op jit(solution)/shard_map/ppermute | solution.py:20
  248.3 189.9 %all-to-all-start.1 = ((bf16[128,96,128]{2,1,0:T(8,128)(2,1)}), bf16[128,96,128]{2,1,0:T(8,128)(2,1)}, u32[]{:S(2)}, u32[]{:S(2)}) async-start(bf16[128,96,128]{2,1,0:T(8,128)(2,1)} %bitcast.91), calls=%async_computation.1 | async-start | bytes 6291456 | tf_op jit(solution)/shard_map/all_to_all | solution.py:202
  261.0 173.9 %all-reduce.3.cloned.1.call-start = ((), (), s32[]{:S(2)}) async-start(), calls=%async_computation.2 | async-start | bytes 1048576 | tf_op jit(solution)/shard_map/psum | solution.py:168
  272.4 20.4 %copy-start.4 = (bf16[8,384,128]{2,1,0:T(8,128)(2,1)S(1)}, bf16[8,384,128]{2,1,0:T(8,128)(2,1)}, u32[]{:S(2)}) copy-start(bf16[8,384,128]{2,1,0:T(8,128)(2,1)} %param.17) | copy-start | bytes 2359300
  272.4 20.4 %copy-start.7 = (bf16[3072,512]{1,0:T(8,128)(2,1)S(1)}, bf16[3072,512]{1,0:T(8,128)(2,1)}, u32[]{:S(2)}) copy-start(bf16[3072,512]{1,0:T(8,128)(2,1)} %get-tuple-element.17) | copy-start | bytes 9437188
  272.4 20.4 %copy-start.12 = (f32[3072]{0:T(1024)S(1)}, f32[3072]{0:T(1024)}, u32[]{:S(2)}) copy-start(f32[3072]{0:T(1024)} %copy-done.11) | copy-start | bytes 36868
  272.4 20.4 %copy-start.25 = (f32[128]{0:T(128)S(1)}, f32[128]{0:T(128)}, u32[]{:S(2)}) copy-start(f32[128]{0:T(128)} %param.29) | copy-start | bytes 1540
  272.4 20.4 %copy-start.27 = (bf16[512,128]{1,0:T(8,128)(2,1)S(1)}, bf16[512,128]{1,0:T(8,128)(2,1)}, u32[]{:S(2)}) copy-start(bf16[512,128]{1,0:T(8,128)(2,1)} %param.27) | copy-start | bytes 393220
  272.5 20.4 %copy-start.30 = (f32[128]{0:T(128)S(1)}, f32[128]{0:T(128)}, u32[]{:S(2)}) copy-start(f32[128]{0:T(128)} %param.28) | copy-start | bytes 1540
  (19 other events, 90.1 us)
Sparse Core Ops, SparseCore 0:
  267.3 167.4 all-reduce.2
where the time goes:
time: 532 us; the launch traced here: 523 us
  local copies, waits for them, and re-layouts  164 us (31%)
  other arithmetic  115 us (22%)
  waiting for transfers between devices  79 us (15%)
  blocking collectives  68 us (13%)
  matrix products  43.6 us (8%)
  starting transfers between devices  39.1 us (7%)
  between operations  15.1 us (3%)
    scatter-add x1, other arithmetic, on_device(): jax.ops.segment_sum(recv_rows.reshape(-1, channels).astype(jnp.float32),...  78 us
    psum x1, waiting for transfers between devices, on_device(): lax.psum((conv_term, up_term, down_term), ('lat', 'lon'))  71.4 us
    psum x1, blocking collectives, on_device(): lax.psum((conv_term, up_term, down_term), ('lat', 'lon'))  68 us
    scatter x1, local copies, waits for them, and re-layouts, on_device(): jnp.zeros((devices * capacity, channels), jnp.bfloat16).at[slot_index]  55.3 us
    gather x1, local copies, waits for them, and re-layouts, on_device(): sorted_owner = dest_owner[sorting]  34.3 us
    gather x1, local copies, waits for them, and re-layouts, on_device(): atmos_cell[sorting]  34.3 us
    conv_general_dilated x2, matrix products, depthwise(): lax.conv_general_dilated(padded[None], kernel[:, :, None, :], (1, 1), 'VA...  25.8 us
    scatter x1, local copies, waits for them, and re-layouts, on_device(): jnp.zeros((devices * capacity,), jnp.int32).at[slot_index]  23 us
  transfers between devices with their start and end apart: 11, of which 3 were waited for; matrix products, arithmetic and copies ran while one was open for 28% of the time, Pallas kernels for 0%

commit v1 on v0

v1 whole, which is shorter than its diff:
```python
import functools

import jax
import jax.numpy as jnp
from jax import lax
from jax.experimental import pallas as pl
from jax.experimental.pallas import tpu as pltpu
from jax.sharding import PartitionSpec as P

F32 = jnp.float32
BF16 = jnp.bfloat16
I32 = jnp.int32
MESH = pl.DeviceIdType.MESH
VMEM_SPEC = pl.BlockSpec(memory_space=pltpu.VMEM)
SMEM_SPEC = pl.BlockSpec(memory_space=pltpu.SMEM)
ANY_SPEC = pl.BlockSpec(memory_space=pl.ANY)

A_DEV = 512
LANES = 128
CAP = 96
MARGIN = 3
TAPS = 7
LAT = 8
LON = 16
DEVICES = LAT * LON
PART_ROWS = 144

gelu_scale = 0.7978845608028654
cubic_coef = 0.044715


def nt_dot(a, b):
    return lax.dot_general(a, b, (((1,), (1,)), ((), ())), preferred_element_type=F32)


def nn_dot(a, b):
    return jnp.dot(a, b, preferred_element_type=F32)


def rank_kernel(owner_ref, cell_ref, index_ref, table_ref, slot_ref, weight_ref, cells_ref, base, acc):
    blocks = owner_ref.shape[0]
    group = 8
    base[...] = jnp.zeros_like(base)
    acc[...] = jnp.zeros_like(acc)
    row_id = lax.broadcasted_iota(I32, (LANES, LANES), 0)
    col_id = lax.broadcasted_iota(I32, (LANES, LANES), 1)
    tri = jnp.concatenate(
        [jnp.where(row_id < col_id, 1.0, 0.0), jnp.ones((LANES, LANES), F32)], axis=1
    ).astype(BF16)

    index = index_ref[...]
    weight = jnp.zeros(index.shape, F32)
    for entry in range(table_ref.shape[0]):
        weight = jnp.where(index == entry, table_ref[entry], weight)
    weight_ref[...] = weight

    def body(step, carry):
        start = pl.multiple_of(step * group, group)
        owners = owner_ref[pl.ds(start, group), :]
        coded = cell_ref[pl.ds(start, group), :] + 1
        high = (coded >> 1).astype(F32)
        low = (coded & 1).astype(F32)
        ranks = []
        for i in range(group):
            hit = row_id == owners[i : i + 1, :]
            hot = jnp.where(hit, 1.0, 0.0)
            hot16 = hot.astype(BF16)
            sums = nn_dot(hot16, tri)
            before = sums[:, :LANES] + base[...]
            rank = jnp.sum(hot * before, axis=0, keepdims=True)
            ranks.append(rank)
            base[...] += sums[:, LANES:]
            at_rank = row_id == rank.astype(I32)
            spread = jnp.concatenate(
                [
                    jnp.where(at_rank, high[i : i + 1, :], 0.0),
                    jnp.where(at_rank, low[i : i + 1, :], 0.0),
                ],
                axis=0,
            ).astype(BF16)
            acc[...] += nt_dot(hot16, spread)
        rank8 = jnp.concatenate(ranks, axis=0).astype(I32)
        slot_ref[pl.ds(start, group), :] = owners * CAP + rank8
        return carry

    lax.fori_loop(0, blocks // group, body, 0)
    total = acc[...]
    cells_ref[...] = (2.0 * total[:, :LANES] + total[:, LANES:]).astype(I32) - 1


def rank_entries(owner, atmos_cell, weight_index, table):
    entries = owner.shape[0]
    shape = (entries // LANES, LANES)
    return pl.pallas_call(
        rank_kernel,
        out_shape=(
            jax.ShapeDtypeStruct(shape, I32),
            jax.ShapeDtypeStruct(shape, F32),
            jax.ShapeDtypeStruct((DEVICES, LANES), I32),
        ),
        in_specs=[VMEM_SPEC, VMEM_SPEC, VMEM_SPEC, SMEM_SPEC],
        out_specs=[VMEM_SPEC, VMEM_SPEC, VMEM_SPEC],
        scratch_shapes=[pltpu.VMEM((LANES, LANES), F32), pltpu.VMEM((LANES, 2 * LANES), F32)],
        name="rank_entries",
        cost_estimate=pl.CostEstimate(flops=10**9, bytes_accessed=10**6, transcendentals=0),
    )(owner.reshape(shape), atmos_cell.reshape(shape), weight_index.reshape(shape), table)


def block_kernel(
    padded_ref,
    state_ref,
    forcing_ref,
    cot_ref,
    land_ref,
    dw_ref,
    chan_ref,
    up_ref,
    up_bias_ref,
    down_ref,
    slot_ref,
    weight_ref,
    result_ref,
    parts_ref,
    send_ref,
    xf,
    wts,
    conv,
    gconv,
    gm,
    pre,
    gh,
    hid,
    gp,
    norm,
    up_acc,
    down_acc,
    buf,
):
    rows, cols, channels = state_ref.shape
    hidden_units = up_ref.shape[1]
    dw_bias = chan_ref[0:1, :]
    gain = chan_ref[1:2, :]
    shift = chan_ref[2:3, :]
    down_bias = chan_ref[3:4, :]
    scale = chan_ref[4:5, :]

    def zero_body(i, carry):
        buf[pl.ds(pl.multiple_of(i * 128, 128), 128), :] = jnp.zeros((128, channels), F32)
        return carry

    lax.fori_loop(0, buf.shape[0] // 128, zero_body, 0)
    up_acc[...] = jnp.zeros_like(up_acc)
    down_acc[...] = jnp.zeros_like(down_acc)

    def unpack(i, carry):
        xf[i] = padded_ref[i].astype(F32)
        return carry

    lax.fori_loop(0, rows + 2 * MARGIN, unpack, 0)
    for tap in range(TAPS * TAPS):
        wts[tap] = jnp.broadcast_to(dw_ref[tap : tap + 1, :], (8, channels))

    def conv_body(block, carry):
        start = block * 8
        total = [jnp.broadcast_to(dw_bias, (8, channels)) for _ in range(rows)]
        for b in range(TAPS):
            xs = [xf[line, pl.ds(start + b, 8), :] for line in range(rows + TAPS - 1)]
            for a in range(TAPS):
                wv = wts[a * TAPS + b]
                for r in range(rows):
                    total[r] = total[r] + xs[r + a] * wv
        for r in range(rows):
            conv[r, pl.ds(pl.multiple_of(start, 8), 8), :] = total[r]
        return carry

    lax.fori_loop(0, cols // 8, conv_body, 0)

    land = land_ref[...].astype(F32)
    line_id = lax.broadcasted_iota(I32, land.shape, 0)
    ones = jnp.ones((rows, channels), BF16)

    def tile_body(r, carry):
        field = conv[r]
        centred = field - jnp.mean(field, axis=-1, keepdims=True)
        inv_std = lax.rsqrt(jnp.mean(centred * centred, axis=-1, keepdims=True) + 1e-06)
        normed = centred * inv_std
        norm[...] = normed
        mixed = (normed * gain + shift + forcing_ref[r].astype(F32)).astype(BF16)
        own_line = jnp.where(line_id == r, land, 0.0).astype(BF16)
        ocean = lax.dot_general(
            own_line, ones, (((0,), (0,)), ((), ())), preferred_element_type=F32
        )
        grad_out = (ocean * scale * cot_ref[r].astype(F32)).astype(BF16)
        pre[...] = nn_dot(mixed, up_ref[...]) + up_bias_ref[...]
        gh[...] = nt_dot(grad_out, down_ref[...])

        def gelu_body(i, carry):
            start = pl.multiple_of(i * 16, 16)
            p = pre[pl.ds(start, 16), :]
            u = p * p
            half = 0.5 + 0.5 * jnp.tanh(p * (gelu_scale + gelu_scale * cubic_coef * u))
            value = p * half
            slope = half + value * (1.0 - half) * (
                2.0 * gelu_scale + 6.0 * gelu_scale * cubic_coef * u
            )
            hid[pl.ds(start, 16), :] = value.astype(BF16)
            gp[pl.ds(start, 16), :] = (gh[pl.ds(start, 16), :] * slope).astype(BF16)
            return carry

        lax.fori_loop(0, cols // 16, gelu_body, 0)
        hidden = hid[...]
        grad_pre = gp[...]
        projected = nn_dot(hidden, down_ref[...]) + down_bias
        result_ref[r] = (ocean * (state_ref[r].astype(F32) + scale * projected)).astype(BF16)
        down_acc[...] += nn_dot(grad_out.T, hidden)
        up_acc[...] += nn_dot(mixed.T, grad_pre)
        grad_mixed = nt_dot(grad_pre, up_ref[...])
        gm[pl.ds(pl.multiple_of(r * cols, cols), cols), :] = grad_mixed
        gained = grad_mixed * gain
        normed2 = norm[...]
        back = (
            gained
            - jnp.mean(gained, axis=-1, keepdims=True)
            - normed2 * jnp.mean(gained * normed2, axis=-1, keepdims=True)
        ) * inv_std
        gconv[r] = back.astype(BF16).astype(F32)
        return carry

    lax.fori_loop(0, rows, tile_body, 0)

    unit = 8

    def pack_body(i, carry):
        first = i * unit
        for k in range(unit):
            line = gm[pl.ds(first + k, 1), :]
            for j in range(2):
                entry = 2 * first + 2 * k + j
                buf[pl.ds(slot_ref[entry], 1), :] = line * weight_ref[entry]
        return carry

    lax.fori_loop(0, rows * cols // unit, pack_body, 0)

    for blk in range(hidden_units // LANES):
        parts_ref[blk, 0:LANES, :] = up_acc[:, blk * LANES : (blk + 1) * LANES].astype(BF16)
        parts_ref[4 + blk, 0:LANES, :] = down_acc[:, blk * LANES : (blk + 1) * LANES].T.astype(BF16)
    parts_ref[TAPS, LANES:, :] = jnp.zeros((PART_ROWS - LANES, channels), BF16)

    sums = [[None] * TAPS for _ in range(TAPS)]
    for b in range(TAPS):

        def corr_body(block, carry):
            start = block * 8
            xs = [xf[line, pl.ds(start + b, 8), :] for line in range(rows + TAPS - 1)]
            gs = [gconv[r, pl.ds(pl.multiple_of(start, 8), 8), :] for r in range(rows)]
            out = []
            for a in range(TAPS):
                total = carry[a]
                for r in range(rows):
                    total = total + xs[r + a] * gs[r]
                out.append(total)
            return tuple(out)

        done = lax.fori_loop(
            0, cols // 8, corr_body, tuple(jnp.zeros((8, channels), F32) for _ in range(TAPS))
        )
        for a in range(TAPS):
            sums[a][b] = jnp.sum(done[a], axis=0, keepdims=True)
    for a in range(TAPS):
        lines = sums[a] + [jnp.zeros((PART_ROWS - LANES - TAPS, channels), F32)]
        parts_ref[a, LANES:, :] = jnp.concatenate(lines, axis=0).astype(BF16)

    def cast_body(i, carry):
        send_ref[i] = buf[pl.ds(pl.multiple_of(i * CAP, CAP), CAP), :].astype(BF16)
        return carry

    lax.fori_loop(0, DEVICES, cast_body, 0)


def run_block(padded, state, forcing, cotangent, land, dw, chan, up, up_bias, down, slots, weights):
    rows, cols, channels = state.shape
    hidden = up.shape[1]
    wide = padded.shape[1]
    lines = padded.shape[0]
    return pl.pallas_call(
        block_kernel,
        out_shape=(
            jax.ShapeDtypeStruct(state.shape, BF16),
            jax.ShapeDtypeStruct((LAT, PART_ROWS, LANES), BF16),
            jax.ShapeDtypeStruct((DEVICES, CAP, channels), BF16),
        ),
        in_specs=[VMEM_SPEC] * 10 + [SMEM_SPEC] * 2,
        out_specs=[VMEM_SPEC] * 3,
        scratch_shapes=[
            pltpu.VMEM((lines, wide, channels), F32),
            pltpu.VMEM((TAPS * TAPS, 8, channels), F32),
            pltpu.VMEM((rows, cols, channels), F32),
            pltpu.VMEM((rows, cols, channels), F32),
            pltpu.VMEM((rows * cols, channels), F32),
            pltpu.VMEM((cols, hidden), F32),
            pltpu.VMEM((cols, hidden), F32),
            pltpu.VMEM((cols, hidden), BF16),
            pltpu.VMEM((cols, hidden), BF16),
            pltpu.VMEM((cols, channels), F32),
            pltpu.VMEM((channels, hidden), F32),
            pltpu.VMEM((channels, hidden), F32),
            pltpu.VMEM((DEVICES * CAP, channels), F32),
        ],
        name="block_pass",
        cost_estimate=pl.CostEstimate(
            flops=3 * 10**9, bytes_accessed=10**7, transcendentals=rows * cols * hidden
        ),
    )(padded, state, forcing, cotangent, land, dw, chan, up, up_bias, down, slots, weights)


def exchange_kernel(
    factor,
    rows_hbm,
    cells_hbm,
    parts_ref,
    up_ref,
    down_ref,
    dw_ref,
    grad_ref,
    recv_rows,
    recv_cells,
    recv1,
    send2,
    recv2,
    send3,
    recv3,
    send4,
    recv4,
    row_send,
    row_recv,
    cell_send,
    cell_recv,
    send_sem,
    recv_sem,
):
    lat = lax.axis_index("lat")
    lon = lax.axis_index("lon")
    me = lat * LON + lon

    def device(k):
        peer = lax.rem(me + k, DEVICES)
        return (peer // LON, lax.rem(peer, LON))

    barrier = pltpu.get_barrier_semaphore()

    def greet(k, carry):
        pl.semaphore_signal(barrier, inc=1, device_id=device(k), device_id_type=MESH)
        return carry

    lax.fori_loop(1, DEVICES, greet, 0)

    recv_rows[:, CAP:, :] = jnp.zeros((DEVICES, LANES - CAP, LANES), BF16)
    grad_ref[...] = jnp.zeros_like(grad_ref)
    pl.semaphore_wait(barrier, DEVICES - 1)

    def row_copy(k):
        to = device(k)
        peer = to[0] * LON + to[1]
        return (
            pltpu.make_async_remote_copy(
                src_ref=rows_hbm.at[peer],
                dst_ref=recv_rows.at[k, pl.ds(0, CAP)],
                send_sem=row_send.at[k],
                recv_sem=row_recv.at[k],
                device_id=to,
                device_id_type=MESH,
            ),
            pltpu.make_async_remote_copy(
                src_ref=cells_hbm.at[peer],
                dst_ref=recv_cells.at[k],
                send_sem=cell_send.at[k],
                recv_sem=cell_recv.at[k],
                device_id=to,
                device_id_type=MESH,
            ),
        )

    def send_range(first, last):
        def body(k, carry):
            for copy in row_copy(k):
                copy.start()
            return carry

        lax.fori_loop(first, last, body, 0)

    own_rows = pltpu.make_async_copy(rows_hbm.at[me], recv_rows.at[0, pl.ds(0, CAP)], row_recv.at[0])
    own_cells = pltpu.make_async_copy(cells_hbm.at[me], recv_cells.at[0], cell_recv.at[0])

    def lat_copy(stage, k, src, dst):
        to = lax.rem(lat + k, LAT)
        return pltpu.make_async_remote_copy(
            src_ref=src(to),
            dst_ref=dst.at[k],
            send_sem=send_sem.at[stage, k],
            recv_sem=recv_sem.at[stage, k],
            device_id=(to, lon),
            device_id_type=MESH,
        )

    def lon_copy(stage, k, src, dst):
        to = lax.rem(lon + k, LON)
        return pltpu.make_async_remote_copy(
            src_ref=src(to),
            dst_ref=dst.at[k],
            send_sem=send_sem.at[stage, k],
            recv_sem=recv_sem.at[stage, k],
            device_id=(lat, to),
            device_id_type=MESH,
        )

    def copy1(k):
        return lat_copy(0, k, lambda to: parts_ref.at[to], recv1)

    def copy2(k):
        return lon_copy(1, k, lambda to: send2.at[to], recv2)

    def copy3(k):
        return lon_copy(2, k, lambda to: send3, recv3)

    def copy4(k):
        return lat_copy(3, k, lambda to: send4, recv4)

    def start_all(copy, count):
        def body(k, carry):
            copy(k).start()
            return carry

        lax.fori_loop(1, count, body, 0)

    def arrive_all(copy, count):
        def body(k, carry):
            copy(k).wait_recv()
            return carry

        lax.fori_loop(1, count, body, 0)

    def left_all(copy, count):
        def body(k, carry):
            copy(k).wait_send()
            return carry

        lax.fori_loop(1, count, body, 0)

    start_all(copy1, LAT)
    own_rows.start()
    own_cells.start()
    send_range(1, 32)
    arrive_all(copy1, LAT)
    total = parts_ref[lat].astype(F32)
    for k in range(1, LAT):
        total = total + recv1[k].astype(F32)
    tail = total[LANES : LANES + 8, :]
    for j in range(LON):
        send2[j] = jnp.concatenate([total[8 * j : 8 * j + 8, :], tail], axis=0).astype(BF16)

    start_all(copy2, LON)
    send_range(32, 64)
    arrive_all(copy2, LON)
    total = send2[lon].astype(F32)
    for k in range(1, LON):
        total = total + recv2[k].astype(F32)
    send3[...] = total[:8, :]
    send4[LANES:, :] = jnp.concatenate([total[8:, :], jnp.zeros((8, LANES), F32)], axis=0).astype(BF16)

    start_all(copy3, LON)
    send_range(64, 96)
    arrive_all(copy3, LON)
    recv3[0] = send3[...]
    for j in range(LON // 2):
        pair = [recv3[lax.rem(lon - (2 * j + i) + LON, LON)] for i in range(2)]
        send4[16 * j : 16 * j + 16, :] = jnp.concatenate(pair, axis=0).astype(BF16)

    start_all(copy4, LAT)
    send_range(96, DEVICES)

    cell_id = lax.broadcasted_iota(I32, (A_DEV, LANES), 0)

    def add_pair(i):
        hot = jnp.concatenate(
            [jnp.where(cell_id == recv_cells[2 * i + j], 1.0, 0.0).astype(BF16) for j in range(2)],
            axis=1,
        )
        values = recv_rows[pl.ds(2 * i, 2)].reshape(2 * LANES, LANES)
        grad_ref[...] += nn_dot(hot, values)

    def wait_rows(k):
        for copy in row_copy(k):
            copy.wait_recv()

    own_rows.wait()
    own_cells.wait()
    wait_rows(1)
    add_pair(0)

    def pair_body(i, carry):
        wait_rows(2 * i)
        wait_rows(2 * i + 1)
        add_pair(i)
        return carry

    lax.fori_loop(1, DEVICES // 2, pair_body, 0)

    arrive_all(copy4, LAT)
    recv4[0] = send4[...]
    for chunk in range(LAT):
        block = recv4[lax.rem(lat - chunk + LAT, LAT)].astype(F32) * factor
        if chunk < 4:
            up_ref[:, chunk * LANES : (chunk + 1) * LANES] = block[:LANES]
        else:
            down_ref[(chunk - 4) * LANES : (chunk - 3) * LANES, :] = block[:LANES]
        if chunk < TAPS:
            dw_ref[chunk] = block[LANES : LANES + TAPS]

    left_all(copy1, LAT)
    left_all(copy2, LON)
    left_all(copy3, LON)
    left_all(copy4, LAT)

    def left_body(k, carry):
        for copy in row_copy(k):
            copy.wait_send()
        return carry

    lax.fori_loop(1, DEVICES, left_body, 0)


def exchange(rows, cells, parts, factor):
    dma = pltpu.SemaphoreType.DMA
    return pl.pallas_call(
        functools.partial(exchange_kernel, factor),
        out_shape=(
            jax.ShapeDtypeStruct((LANES, 512), F32),
            jax.ShapeDtypeStruct((512, LANES), F32),
            jax.ShapeDtypeStruct((TAPS, TAPS, LANES), F32),
            jax.ShapeDtypeStruct((A_DEV, LANES), F32),
        ),
        in_specs=[ANY_SPEC, ANY_SPEC, VMEM_SPEC],
        out_specs=[VMEM_SPEC] * 4,
        scratch_shapes=[
            pltpu.VMEM((DEVICES, LANES, LANES), BF16),
            pltpu.VMEM((DEVICES, 1, LANES), I32),
            pltpu.VMEM((LAT, PART_ROWS, LANES), BF16),
            pltpu.VMEM((LON, 16, LANES), BF16),
            pltpu.VMEM((LON, 16, LANES), BF16),
            pltpu.VMEM((8, LANES), F32),
            pltpu.VMEM((LON, 8, LANES), F32),
            pltpu.VMEM((PART_ROWS, LANES), BF16),
            pltpu.VMEM((LAT, PART_ROWS, LANES), BF16),
            dma((DEVICES,)),
            dma((DEVICES,)),
            dma((DEVICES,)),
            dma((DEVICES,)),
            dma((4, LON)),
            dma((4, LON)),
        ],
        compiler_params=pltpu.CompilerParams(collective_id=0, has_side_effects=True),
        name="exchange",
    )(rows, cells.reshape(DEVICES, 1, LANES), parts)


def extended(block, sides, width, periodic):
    for axis, dim in sides:
        count = lax.axis_size(axis)
        forward = [(i, i + 1) for i in range(count - 1)]
        if periodic:
            forward.append((count - 1, 0))
        backward = [(target, source) for source, target in forward]
        low = lax.ppermute(
            lax.slice_in_dim(block, block.shape[dim] - width, None, axis=dim), axis, forward
        )
        high = lax.ppermute(lax.slice_in_dim(block, 0, width, axis=dim), axis, backward)
        block = jnp.concatenate([low, block, high], axis=dim)
    return block


def on_device(
    state,
    forcing,
    cotangent,
    land_mask,
    dw_weight,
    dw_bias,
    norm_gain,
    norm_bias,
    up_weight,
    up_bias,
    down_weight,
    down_bias,
    layer_scale,
    owner,
    atmos_cell,
    weight_index,
    intersection_weights,
):
    rows, cols, channels = state.shape
    slots, weights, cells = rank_entries(owner[:, 0], atmos_cell, weight_index, intersection_weights)

    lon_ext = extended(state, (("lon", 1),), MARGIN, True)
    padded = extended(lon_ext, (("lat", 0),), MARGIN, False)
    partner = lax.ppermute(
        lon_ext[rows - MARGIN :], "lon", [(i, LON - 1 - i) for i in range(LON)]
    )
    mirrored = partner[::-1, ::-1]
    northmost = lax.axis_index("lat") == LAT - 1
    north_rows = jnp.where(northmost, mirrored, padded[rows + MARGIN :])
    padded = jnp.concatenate([padded[: rows + MARGIN], north_rows], axis=0)
    padded = jnp.pad(padded, ((0, 0), (0, 2), (0, 0)))

    chan = jnp.stack(
        [dw_bias, norm_gain, norm_bias, down_bias, layer_scale] + [jnp.zeros_like(dw_bias)] * 3
    )
    result, parts, send_rows = run_block(
        padded,
        state,
        forcing,
        cotangent,
        land_mask,
        dw_weight.astype(F32).reshape(TAPS * TAPS, channels),
        chan,
        up_weight,
        up_bias.reshape(1, -1),
        down_weight,
        slots.reshape(-1),
        weights.reshape(-1),
    )
    factor = float(rows * LAT * cols * LON) ** (-0.5)
    grad_up, grad_down, grad_dw, forcing_grad = exchange(send_rows, cells, parts, factor)
    return (result, grad_dw, grad_up, grad_down, forcing_grad)


def solution(mesh):
    in_specs = (
        P("lat", "lon", None),
        P("lat", "lon", None),
        P("lat", "lon", None),
        P("lat", "lon"),
        P(),
        P(),
        P(),
        P(),
        P(),
        P(),
        P(),
        P(),
        P(),
        P(("lat", "lon"), None),
        P(("lat", "lon")),
        P(("lat", "lon")),
        P(),
    )
    out_specs = (P("lat", "lon", None), P(), P(), P(), P(("lat", "lon"), None))
    return jax.shard_map(
        on_device, mesh=mesh, in_specs=in_specs, out_specs=out_specs, check_vma=False
    )
```

time: 532 us -> 167 us (0.31)
  the two profiles are of different devices: /device:TPU:1 before, /device:TPU:65 now
where the time goes in v1:
time: 167 us
  Pallas kernels  138 us (83%)
  starting transfers between devices  11.1 us (7%)
  local copies, waits for them, and re-layouts  9.41 us (6%)
  waiting for transfers between devices  4.58 us (3%)
  other arithmetic  2.65 us (2%)
    pallas_call x1, Pallas kernels, exchange(): pl.pallas_call(functools.partial(exchange_kernel, factor), out_shape=(jax...  87.5 us
    pallas_call x1, Pallas kernels, run_block(): pl.pallas_call(block_kernel, out_shape=(jax.ShapeDtypeStruct(state.shape,...  45.4 us
    ppermute x2, starting transfers between devices, extended(): lax.ppermute(lax.slice_in_dim(block, block.shape[dim] - width, None, axis...  6.89 us
    unnamed x18, local copies, waits for them, and re-layouts  6.4 us
    pallas_call x1, Pallas kernels, rank_entries(): pl.pallas_call(rank_kernel, out_shape=(jax.ShapeDtypeStruct(shape, I32),...  5.07 us
    ppermute x2, waiting for transfers between devices, extended(): lax.ppermute(lax.slice_in_dim(block, 0, width, axis=dim), axis, backward)  3.79 us
  transfers between devices with their start and end apart: 5, of which 2 were waited for; matrix products, arithmetic and copies ran while one was open for 1% of the time, Pallas kernels for 3%

profile of v1, /device:TPU:65, one launch (start us, length us, event | category | flops | bytes accessed | tf_op | source)
XLA Modules:
  0.0 166.6 jit_solution(17596481188386067156)
XLA Ops:
  0.7 0.8 fusion.9
  1.5 3.5 %collective-permute-start = (bf16[8,3,128]{2,1,0:T(4,128)(2,1)S(1)}, bf16[8,3,128]{2,1,0:T(4,128)(2,1)S(1)}, u32[]{:S(2)}, u32[]{:S(2)}) collective-permute-start(bf16[8,3,128]{2,1,0:T(4,128)(2,1)S(1)} %get-tuple-element.27), channel_id=1, source_target_pairs={{0,1},{1,2},{2,3},{3,4},{4,5},{5,6},{6,7},{7,8},{8,9},{9,10},{10,1... | collective-permute-start | bytes 18440 | tf_op jit(solution)/shard_map/ppermute | solution.py:573
  5.0 0.8 collective-permute-done
  5.8 3.8 %collective-permute-done.1 = bf16[8,3,128]{2,1,0:T(4,128)(2,1)S(1)} collective-permute-done((bf16[8,3,128]{2,1,0:T(4,128)(2,1)S(1)}, bf16[8,3,128]{2,1,0:T(4,128)(2,1)S(1)}, u32[]{:S(2)}, u32[]{:S(2)}) %collective-permute-start.1) | collective-permute-done | bytes 6176 | tf_op jit(solution)/shard_map/ppermute | solution.py:576
  9.6 1.2 pad_maximum_fusion
  10.8 2.3 %collective-permute-start.3 = (bf16[3,390,128]{2,1,0:T(8,128)(2,1)S(1)}, bf16[3,390,128]{2,1,0:T(8,128)(2,1)S(1)}, u32[]{:S(2)}, u32[]{:S(2)}) collective-permute-start(bf16[3,390,128]{2,1,0:T(8,128)(2,1)S(1)} %get-tuple-element.26), channel_id=1, source_target_pairs={{0,15},{1,14},{2,13},{3,12},{4,11},{5,10},{6,9},{7,8},{8,7},{9,6},... | collective-permute-start | bytes 898568 | tf_op jit(solution)/shard_map/ppermute | solution.py:605
  13.1 1.9 %collective-permute-start.4 = (bf16[3,390,128]{2,1,0:T(8,128)(2,1)S(1)}, bf16[3,390,128]{2,1,0:T(8,128)(2,1)S(1)}, u32[]{:S(2)}, u32[]{:S(2)}) collective-permute-start(bf16[3,390,128]{2,1,0:T(8,128)(2,1)S(1)} %get-tuple-element.25), channel_id=1, source_target_pairs={{16,0},{32,16},{48,32},{64,48},{80,64},{96,80},{112,96},{17,1},{33... | collective-permute-start | bytes 898568 | tf_op jit(solution)/shard_map/ppermute | solution.py:576
  15.1 0.6 reshape.42.dw_ref
  15.7 0.6 stack.27.chan_ref
  16.3 3.4 %collective-permute-start.2 = (bf16[3,390,128]{2,1,0:T(8,128)(2,1)S(1)}, bf16[3,390,128]{2,1,0:T(8,128)(2,1)S(1)}, u32[]{:S(2)}, u32[]{:S(2)}) collective-permute-start(bf16[3,390,128]{2,1,0:T(8,128)(2,1)S(1)} %get-tuple-element.26), channel_id=1, source_target_pairs={{0,16},{16,32},{32,48},{48,64},{64,80},{80,96},{96,112},{1,17},{17... | collective-permute-start | bytes 898568 | tf_op jit(solution)/shard_map/ppermute | solution.py:573
  19.7 5.1 %rank_entries.1 = (s32[48,128]{1,0:T(8,128)}, f32[48,128]{1,0:T(8,128)}, s32[128,128]{1,0:T(8,128)}) custom-call(s32[48,128]{1,0:T(8,128)} %bitcast.18, s32[48,128]{1,0:T(8,128)} %bitcast.19, s32[48,128]{1,0:T(8,128)} %bitcast.20, f32[16]{0:T(128)} %table_ref.1), custom_call_target="tpu_custom_call" | custom-call | flops 1000000000 | bytes 1000000 | tf_op jit(solution)/shard_map/rank_entries/pallas_call | solution.py:94
  24.8 0.0 collective-permute-done.3
  24.8 1.0 rev.3
  25.8 0.0 collective-permute-done.4
  25.8 0.1 broadcast_select_fusion
  25.9 0.0 collective-permute-done.2
  25.9 0.0 copy-done
  25.9 1.3 fusion.6.padded_ref
  27.2 45.4 %block_pass.1 = (bf16[8,384,128]{2,1,0:T(8,128)(2,1)}, bf16[8,144,128]{2,1,0:T(8,128)(2,1)}, bf16[128,96,128]{2,1,0:T(8,128)(2,1)}) custom-call(bf16[14,392,128]{2,1,0:T(8,128)(2,1)} %fusion.6.padded_ref, bf16[8,384,128]{2,1,0:T(8,128)(2,1)} %state_ref.1, bf16[8,384,128]{2,1,0:T(8,128)(2,1)} %forcing_ref.1, bf16[8,384,128]{2,1,0:T(8,128)(2,1)} %cot_ref.1, ...), custom_call_target="tpu_custom_call" | custom-call | flops 3000000000 | bytes 10000000 | tf_op jit(solution)/shard_map/block_pass/pallas_call | solution.py:285
  72.7 87.5 %exchange.1 = (f32[128,512]{1,0:T(8,128)}, f32[512,128]{1,0:T(8,128)}, f32[7,7,128]{2,1,0:T(8,128)}, f32[512,128]{1,0:T(8,128)}) custom-call(bf16[128,96,128]{2,1,0:T(8,128)(2,1)} %get-tuple-element.18.rows_hbm, s32[128,1,128]{2,1,0:T(1,128)} %bitcast.12, bf16[8,144,128]{2,1,0:T(8,128)(2,1)} %get-tuple-element.20.parts_ref), custom_call_target="tpu_custom_call" | custom-call | tf_op jit(solution)/shard_map/exchange/pallas_call | solution.py:534
  160.2 1.4 copy.26
  161.6 1.7 %copy.27 = f32[128,512]{1,0:T(8,128)} copy(f32[128,512]{1,0:T(8,128)} %get-tuple-element.36) | data formatting | bytes 524288
  163.3 1.7 %copy.28 = f32[512,128]{1,0:T(8,128)} copy(f32[512,128]{1,0:T(8,128)} %get-tuple-element.37) | data formatting | bytes 524288
  164.9 1.7 %copy.29 = f32[512,128]{1,0:T(8,128)} copy(f32[512,128]{1,0:T(8,128)} %get-tuple-element.38) | data formatting | bytes 524288
  (16 shorter events, 0.0 us)
Async XLA Ops:
  0.6 14.4 %copy-start.1 = (bf16[7,7,128]{2,1,0:T(8,128)(2,1)S(1)}, bf16[7,7,128]{2,1,0:T(8,128)(2,1)}, u32[]{:S(2)}) copy-start(bf16[7,7,128]{2,1,0:T(8,128)(2,1)} %param.21) | copy-start | bytes 37636
  0.6 15.0 %copy-start.6 = (f32[128]{0:T(128)S(1)}, f32[128]{0:T(128)}, u32[]{:S(2)}) copy-start(f32[128]{0:T(128)} %param.29) | copy-start | bytes 1540
  0.7 15.0 %copy-start.5 = (f32[128]{0:T(128)S(1)}, f32[128]{0:T(128)}, u32[]{:S(2)}) copy-start(f32[128]{0:T(128)} %param.28) | copy-start | bytes 1540
  0.7 15.0 %copy-start.4 = (f32[128]{0:T(128)S(1)}, f32[128]{0:T(128)}, u32[]{:S(2)}) copy-start(f32[128]{0:T(128)} %param.24) | copy-start | bytes 1540
  0.7 15.0 %copy-start.3 = (f32[128]{0:T(128)S(1)}, f32[128]{0:T(128)}, u32[]{:S(2)}) copy-start(f32[128]{0:T(128)} %param.23) | copy-start | bytes 1540
  0.7 15.0 %copy-start.2 = (f32[128]{0:T(128)S(1)}, f32[128]{0:T(128)}, u32[]{:S(2)}) copy-start(f32[128]{0:T(128)} %param.22) | copy-start | bytes 1540
  1.5 4.3 %collective-permute-start = (bf16[8,3,128]{2,1,0:T(4,128)(2,1)S(1)}, bf16[8,3,128]{2,1,0:T(4,128)(2,1)S(1)}, u32[]{:S(2)}, u32[]{:S(2)}) collective-permute-start(bf16[8,3,128]{2,1,0:T(4,128)(2,1)S(1)} %get-tuple-element.27), channel_id=1, source_target_pairs={{0,1},{1,2},{2,3},{3,4},{4,5},{5,6},{6,7},{7,8},{8,9},{9,10},{10,1... | collective-permute-start | bytes 18440 | tf_op jit(solution)/shard_map/ppermute | solution.py:573
  5.0 4.6 %collective-permute-start.1 = (bf16[8,3,128]{2,1,0:T(4,128)(2,1)S(1)}, bf16[8,3,128]{2,1,0:T(4,128)(2,1)S(1)}, u32[]{:S(2)}, u32[]{:S(2)}) collective-permute-start(bf16[8,3,128]{2,1,0:T(4,128)(2,1)S(1)} %get-tuple-element.28), channel_id=1, source_target_pairs={{1,0},{2,1},{3,2},{4,3},{5,4},{6,5},{7,6},{8,7},{9,8},{10,9},{11,1... | collective-permute-start | bytes 18440 | tf_op jit(solution)/shard_map/ppermute | solution.py:576
  10.8 14.0 %collective-permute-start.3 = (bf16[3,390,128]{2,1,0:T(8,128)(2,1)S(1)}, bf16[3,390,128]{2,1,0:T(8,128)(2,1)S(1)}, u32[]{:S(2)}, u32[]{:S(2)}) collective-permute-start(bf16[3,390,128]{2,1,0:T(8,128)(2,1)S(1)} %get-tuple-element.26), channel_id=1, source_target_pairs={{0,15},{1,14},{2,13},{3,12},{4,11},{5,10},{6,9},{7,8},{8,7},{9,6},... | collective-permute-start | bytes 898568 | tf_op jit(solution)/shard_map/ppermute | solution.py:605
  13.1 12.7 %collective-permute-start.4 = (bf16[3,390,128]{2,1,0:T(8,128)(2,1)S(1)}, bf16[3,390,128]{2,1,0:T(8,128)(2,1)S(1)}, u32[]{:S(2)}, u32[]{:S(2)}) collective-permute-start(bf16[3,390,128]{2,1,0:T(8,128)(2,1)S(1)} %get-tuple-element.25), channel_id=1, source_target_pairs={{16,0},{32,16},{48,32},{64,48},{80,64},{96,80},{112,96},{17,1},{33... | collective-permute-start | bytes 898568 | tf_op jit(solution)/shard_map/ppermute | solution.py:576
  16.3 9.5 %collective-permute-start.2 = (bf16[3,390,128]{2,1,0:T(8,128)(2,1)S(1)}, bf16[3,390,128]{2,1,0:T(8,128)(2,1)S(1)}, u32[]{:S(2)}, u32[]{:S(2)}) collective-permute-start(bf16[3,390,128]{2,1,0:T(8,128)(2,1)S(1)} %get-tuple-element.26), channel_id=1, source_target_pairs={{0,16},{16,32},{32,48},{48,64},{64,80},{80,96},{96,112},{1,17},{17... | collective-permute-start | bytes 898568 | tf_op jit(solution)/shard_map/ppermute | solution.py:573
  24.8 1.1 copy-start

commit v2 on v1

--- a/solution.py
+++ b/solution.py
@@ -24,6 +24,9 @@
 LON = 16
 DEVICES = LAT * LON
 PART_ROWS = 144
+STRIDE = 77
+DW_ROWS = 16
+CODE_BITS = 9
 
 gelu_scale = 0.7978845608028654
 cubic_coef = 0.044715
@@ -37,7 +40,7 @@
     return jnp.dot(a, b, preferred_element_type=F32)
 
 
-def rank_kernel(owner_ref, cell_ref, index_ref, table_ref, slot_ref, weight_ref, cells_ref, base, acc):
+def rank_kernel(owner_ref, cell_ref, index_ref, slot_ref, cells_ref, base, acc):
     blocks = owner_ref.shape[0]
     group = 8
     base[...] = jnp.zeros_like(base)
@@ -48,18 +51,12 @@
         [jnp.where(row_id < col_id, 1.0, 0.0), jnp.ones((LANES, LANES), F32)], axis=1
     ).astype(BF16)
 
-    index = index_ref[...]
-    weight = jnp.zeros(index.shape, F32)
-    for entry in range(table_ref.shape[0]):
-        weight = jnp.where(index == entry, table_ref[entry], weight)
-    weight_ref[...] = weight
-
     def body(step, carry):
         start = pl.multiple_of(step * group, group)
         owners = owner_ref[pl.ds(start, group), :]
-        coded = cell_ref[pl.ds(start, group), :] + 1
-        high = (coded >> 1).astype(F32)
-        low = (coded & 1).astype(F32)
+        coded = cell_ref[pl.ds(start, group), :] + (index_ref[pl.ds(start, group), :] << CODE_BITS) + 1
+        high = (coded >> 7).astype(F32)
+        low = (coded & 127).astype(F32)
         ranks = []
         for i in range(group):
             hit = row_id == owners[i : i + 1, :]
@@ -85,25 +82,24 @@
 
     lax.fori_loop(0, blocks // group, body, 0)
     total = acc[...]
-    cells_ref[...] = (2.0 * total[:, :LANES] + total[:, LANES:]).astype(I32) - 1
-
-
-def rank_entries(owner, atmos_cell, weight_index, table):
+    cells_ref[...] = (128.0 * total[:, :LANES] + total[:, LANES:]).astype(I32) - 1
+
+
+def rank_entries(owner, atmos_cell, weight_index):
     entries = owner.shape[0]
     shape = (entries // LANES, LANES)
     return pl.pallas_call(
         rank_kernel,
         out_shape=(
             jax.ShapeDtypeStruct(shape, I32),
-            jax.ShapeDtypeStruct(shape, F32),
             jax.ShapeDtypeStruct((DEVICES, LANES), I32),
         ),
-        in_specs=[VMEM_SPEC, VMEM_SPEC, VMEM_SPEC, SMEM_SPEC],
-        out_specs=[VMEM_SPEC, VMEM_SPEC, VMEM_SPEC],
+        in_specs=[VMEM_SPEC, VMEM_SPEC, VMEM_SPEC],
+        out_specs=[VMEM_SPEC, VMEM_SPEC],
         scratch_shapes=[pltpu.VMEM((LANES, LANES), F32), pltpu.VMEM((LANES, 2 * LANES), F32)],
         name="rank_entries",
         cost_estimate=pl.CostEstimate(flops=10**9, bytes_accessed=10**6, transcendentals=0),
-    )(owner.reshape(shape), atmos_cell.reshape(shape), weight_index.reshape(shape), table)
+    )(owner.reshape(shape), atmos_cell.reshape(shape), weight_index.reshape(shape))
 
 
 def block_kernel(
@@ -118,14 +114,13 @@
     up_bias_ref,
     down_ref,
     slot_ref,
-    weight_ref,
     result_ref,
     parts_ref,
     send_ref,
+    gconv_ref,
     xf,
     wts,
     conv,
-    gconv,
     gm,
     pre,
     gh,
@@ -195,19 +190,19 @@
         gh[...] = nt_dot(grad_out, down_ref[...])
 
         def gelu_body(i, carry):
-            start = pl.multiple_of(i * 16, 16)
-            p = pre[pl.ds(start, 16), :]
+            start = pl.multiple_of(i * 64, 64)
+            p = pre[pl.ds(start, 64), :]
             u = p * p
             half = 0.5 + 0.5 * jnp.tanh(p * (gelu_scale + gelu_scale * cubic_coef * u))
             value = p * half
             slope = half + value * (1.0 - half) * (
                 2.0 * gelu_scale + 6.0 * gelu_scale * cubic_coef * u
             )
-            hid[pl.ds(start, 16), :] = value.astype(BF16)
-            gp[pl.ds(start, 16), :] = (gh[pl.ds(start, 16), :] * slope).astype(BF16)
+            hid[pl.ds(start, 64), :] = value.astype(BF16)
+            gp[pl.ds(start, 64), :] = (gh[pl.ds(start, 64), :] * slope).astype(BF16)
             return carry
 
-        lax.fori_loop(0, cols // 16, gelu_body, 0)
+        lax.fori_loop(0, cols // 64, gelu_body, 0)
         hidden = hid[...]
         grad_pre = gp[...]
         projected = nn_dot(hidden, down_ref[...]) + down_bias
@@ -223,12 +218,12 @@
             - jnp.mean(gained, axis=-1, keepdims=True)
             - normed2 * jnp.mean(gained * normed2, axis=-1, keepdims=True)
         ) * inv_std
-        gconv[r] = back.astype(BF16).astype(F32)
+        gconv_ref[r] = back.astype(BF16)
         return carry
 
     lax.fori_loop(0, rows, tile_body, 0)
 
-    unit = 8
+    unit = 16
 
     def pack_body(i, carry):
         first = i * unit
@@ -236,48 +231,26 @@
             line = gm[pl.ds(first + k, 1), :]
             for j in range(2):
                 entry = 2 * first + 2 * k + j
-                buf[pl.ds(slot_ref[entry], 1), :] = line * weight_ref[entry]
+                buf[pl.ds(slot_ref[entry], 1), :] = line
         return carry
 
     lax.fori_loop(0, rows * cols // unit, pack_body, 0)
 
     for blk in range(hidden_units // LANES):
-        parts_ref[blk, 0:LANES, :] = up_acc[:, blk * LANES : (blk + 1) * LANES].astype(BF16)
-        parts_ref[4 + blk, 0:LANES, :] = down_acc[:, blk * LANES : (blk + 1) * LANES].T.astype(BF16)
-    parts_ref[TAPS, LANES:, :] = jnp.zeros((PART_ROWS - LANES, channels), BF16)
-
-    sums = [[None] * TAPS for _ in range(TAPS)]
-    for b in range(TAPS):
-
-        def corr_body(block, carry):
-            start = block * 8
-            xs = [xf[line, pl.ds(start + b, 8), :] for line in range(rows + TAPS - 1)]
-            gs = [gconv[r, pl.ds(pl.multiple_of(start, 8), 8), :] for r in range(rows)]
-            out = []
-            for a in range(TAPS):
-                total = carry[a]
-                for r in range(rows):
-                    total = total + xs[r + a] * gs[r]
-                out.append(total)
-            return tuple(out)
-
-        done = lax.fori_loop(
-            0, cols // 8, corr_body, tuple(jnp.zeros((8, channels), F32) for _ in range(TAPS))
-        )
-        for a in range(TAPS):
-            sums[a][b] = jnp.sum(done[a], axis=0, keepdims=True)
-    for a in range(TAPS):
-        lines = sums[a] + [jnp.zeros((PART_ROWS - LANES - TAPS, channels), F32)]
-        parts_ref[a, LANES:, :] = jnp.concatenate(lines, axis=0).astype(BF16)
+        parts_ref[blk] = up_acc[:, blk * LANES : (blk + 1) * LANES].astype(BF16)
+        parts_ref[4 + blk] = down_acc[:, blk * LANES : (blk + 1) * LANES].T.astype(BF16)
+    group = 8
 
     def cast_body(i, carry):
-        send_ref[i] = buf[pl.ds(pl.multiple_of(i * CAP, CAP), CAP), :].astype(BF16)
-        return carry
-
-    lax.fori_loop(0, DEVICES, cast_body, 0)
-
-
-def run_block(padded, state, forcing, cotangent, land, dw, chan, up, up_bias, down, slots, weights):
+        for k in range(group):
+            start = pl.multiple_of((i * group + k) * CAP, CAP)
+            send_ref[i * group + k] = buf[pl.ds(start, CAP), :].astype(BF16)
+        return carry
+
+    lax.fori_loop(0, DEVICES // group, cast_body, 0)
+
+
+def run_block(padded, state, forcing, cotangent, land, dw, chan, up, up_bias, down, slots):
     rows, cols, channels = state.shape
     hidden = up.shape[1]
     wide = padded.shape[1]
@@ -286,15 +259,15 @@
         block_kernel,
         out_shape=(
             jax.ShapeDtypeStruct(state.shape, BF16),
-            jax.ShapeDtypeStruct((LAT, PART_ROWS, LANES), BF16),
+            jax.ShapeDtypeStruct((LAT, LANES, LANES), BF16),
             jax.ShapeDtypeStruct((DEVICES, CAP, channels), BF16),
+            jax.ShapeDtypeStruct(state.shape, BF16),
         ),
-        in_specs=[VMEM_SPEC] * 10 + [SMEM_SPEC] * 2,
-        out_specs=[VMEM_SPEC] * 3,
+        in_specs=[VMEM_SPEC] * 10 + [SMEM_SPEC],
+        out_specs=[VMEM_SPEC] * 4,
         scratch_shapes=[
             pltpu.VMEM((lines, wide, channels), F32),
             pltpu.VMEM((TAPS * TAPS, 8, channels), F32),
-            pltpu.VMEM((rows, cols, channels), F32),
             pltpu.VMEM((rows, cols, channels), F32),
             pltpu.VMEM((rows * cols, channels), F32),
             pltpu.VMEM((cols, hidden), F32),
@@ -310,21 +283,25 @@
         cost_estimate=pl.CostEstimate(
             flops=3 * 10**9, bytes_accessed=10**7, transcendentals=rows * cols * hidden
         ),
-    )(padded, state, forcing, cotangent, land, dw, chan, up, up_bias, down, slots, weights)
+    )(padded, state, forcing, cotangent, land, dw, chan, up, up_bias, down, slots)
 
 
 def exchange_kernel(
-    factor,
     rows_hbm,
     cells_hbm,
     parts_ref,
-    up_ref,
-    down_ref,
-    dw_ref,
+    padded_ref,
+    gconv_ref,
+    table_ref,
+    chunks_ref,
     grad_ref,
+    xf,
+    gf,
     recv_rows,
     recv_cells,
     recv1,
+    dw_part,
+    recv_dw,
     send2,
     recv2,
     send3,
@@ -337,26 +314,41 @@
     cell_recv,
     send_sem,
     recv_sem,
+    entered,
 ):
     lat = lax.axis_index("lat")
     lon = lax.axis_index("lon")
     me = lat * LON + lon
 
     def device(k):
-        peer = lax.rem(me + k, DEVICES)
+        peer = lax.rem(me + k * STRIDE, DEVICES)
         return (peer // LON, lax.rem(peer, LON))
 
     barrier = pltpu.get_barrier_semaphore()
 
-    def greet(k, carry):
-        pl.semaphore_signal(barrier, inc=1, device_id=device(k), device_id_type=MESH)
-        return carry
-
-    lax.fori_loop(1, DEVICES, greet, 0)
+    def greet_lon(k, carry):
+        to = (lat, lax.rem(lon + k, LON))
+        pl.semaphore_signal(barrier, inc=1, device_id=to, device_id_type=MESH)
+        return carry
+
+    def greet_lat(k, carry):
+        to = (lax.rem(lat + k, LAT), lon)
+        pl.semaphore_signal(barrier, inc=1, device_id=to, device_id_type=MESH)
+        return carry
+
+    def pass_on(k, carry):
+        to = (lax.rem(lat + k, LAT), lon)
+        pl.semaphore_signal(entered, inc=1, device_id=to, device_id_type=MESH)
+        return carry
+
+    lax.fori_loop(1, LON, greet_lon, 0)
+    lax.fori_loop(1, LAT, greet_lat, 0)
 
     recv_rows[:, CAP:, :] = jnp.zeros((DEVICES, LANES - CAP, LANES), BF16)
     grad_ref[...] = jnp.zeros_like(grad_ref)
-    pl.semaphore_wait(barrier, DEVICES - 1)
+    pl.semaphore_wait(barrier, LON + LAT - 2)
+    lax.fori_loop(1, LAT, pass_on, 0)
+    pl.semaphore_wait(entered, LAT - 1)
 
     def row_copy(k):
         to = device(k)
@@ -416,6 +408,9 @@
     def copy1(k):
         return lat_copy(0, k, lambda to: parts_ref.at[to], recv1)
 
+    def copy_dw(k):
+        return lat_copy(4, k, lambda to: dw_part.at[to], recv_dw)
+
     def copy2(k):
         return lon_copy(1, k, lambda to: send2.at[to], recv2)
 
@@ -449,17 +444,61 @@
     start_all(copy1, LAT)
     own_rows.start()
     own_cells.start()
-    send_range(1, 32)
+    send_range(1, 40)
+
+    lines, wide, channels = xf.shape
+    out_lines, cols = gf.shape[0], gf.shape[1]
+
+    def unpack_x(i, carry):
+        xf[i] = padded_ref[i].astype(F32)
+        return carry
+
+    def unpack_g(i, carry):
+        gf[i] = gconv_ref[i].astype(F32)
+        return carry
+
+    lax.fori_loop(0, lines, unpack_x, 0)
+    lax.fori_loop(0, out_lines, unpack_g, 0)
+    sums = [[None] * TAPS for _ in range(TAPS)]
+    for b in range(TAPS):
+
+        def corr_body(block, carry):
+            start = block * 8
+            xs = [xf[line, pl.ds(start + b, 8), :] for line in range(lines)]
+            gs = [gf[r, pl.ds(pl.multiple_of(start, 8), 8), :] for r in range(out_lines)]
+            out = []
+            for a in range(TAPS):
+                total = carry[a]
+                for r in range(out_lines):
+                    total = total + xs[r + a] * gs[r]
+                out.append(total)
+            return tuple(out)
+
+        done = lax.fori_loop(
+            0, cols // 8, corr_body, tuple(jnp.zeros((8, channels), F32) for _ in range(TAPS))
+        )
+        for a in range(TAPS):
+            sums[a][b] = jnp.sum(done[a], axis=0, keepdims=True)
+    for a in range(TAPS):
+        lines_a = sums[a] + [jnp.zeros((DW_ROWS - TAPS, channels), F32)]
+        dw_part[a] = jnp.concatenate(lines_a, axis=0).astype(BF16)
+    dw_part[TAPS] = jnp.zeros((DW_ROWS, channels), BF16)
+
+    start_all(copy_dw, LAT)
+    send_range(40, 64)
     arrive_all(copy1, LAT)
+    arrive_all(copy_dw, LAT)
     total = parts_ref[lat].astype(F32)
+    tail = dw_part[lat].astype(F32)
     for k in range(1, LAT):
         total = total + recv1[k].astype(F32)
-    tail = total[LANES : LANES + 8, :]
+        tail = tail + recv_dw[k].astype(F32)
+    tail = tail[:8, :]
     for j in range(LON):
         send2[j] = jnp.concatenate([total[8 * j : 8 * j + 8, :], tail], axis=0).astype(BF16)
 
     start_all(copy2, LON)
-    send_range(32, 64)
+    send_range(64, 88)
     arrive_all(copy2, LON)
     total = send2[lon].astype(F32)
     for k in range(1, LON):
@@ -468,7 +507,7 @@
     send4[LANES:, :] = jnp.concatenate([total[8:, :], jnp.zeros((8, LANES), F32)], axis=0).astype(BF16)
 
     start_all(copy3, LON)
-    send_range(64, 96)
+    send_range(88, DEVICES)
     arrive_all(copy3, LON)
     recv3[0] = send3[...]
     for j in range(LON // 2):
@@ -476,15 +515,20 @@
         send4[16 * j : 16 * j + 16, :] = jnp.concatenate(pair, axis=0).astype(BF16)
 
     start_all(copy4, LAT)
-    send_range(96, DEVICES)
 
     cell_id = lax.broadcasted_iota(I32, (A_DEV, LANES), 0)
 
     def add_pair(i):
-        hot = jnp.concatenate(
-            [jnp.where(cell_id == recv_cells[2 * i + j], 1.0, 0.0).astype(BF16) for j in range(2)],
-            axis=1,
-        )
+        parts = []
+        for j in range(2):
+            code = recv_cells[2 * i + j]
+            index = code >> CODE_BITS
+            weight = jnp.zeros(code.shape, F32)
+            for entry in range(table_ref.shape[0]):
+                weight = jnp.where(index == entry, table_ref[entry], weight)
+            cell = jnp.where(code < 0, -1, code & (A_DEV - 1))
+            parts.append(jnp.where(cell_id == cell, weight, 0.0).astype(BF16))
+        hot = jnp.concatenate(parts, axis=1)
         values = recv_rows[pl.ds(2 * i, 2)].reshape(2 * LANES, LANES)
         grad_ref[...] += nn_dot(hot, values)
 
@@ -508,15 +552,10 @@
     arrive_all(copy4, LAT)
     recv4[0] = send4[...]
     for chunk in range(LAT):
-        block = recv4[lax.rem(lat - chunk + LAT, LAT)].astype(F32) * factor
-        if chunk < 4:
-            up_ref[:, chunk * LANES : (chunk + 1) * LANES] = block[:LANES]
-        else:
-            down_ref[(chunk - 4) * LANES : (chunk - 3) * LANES, :] = block[:LANES]
-        if chunk < TAPS:
-            dw_ref[chunk] = block[LANES : LANES + TAPS]
+        chunks_ref[chunk] = recv4[lax.rem(lat - chunk + LAT, LAT)]
 
     left_all(copy1, LAT)
+    left_all(copy_dw, LAT)
     left_all(copy2, LON)
     left_all(copy3, LON)
     left_all(copy4, LAT)
@@ -529,22 +568,24 @@
     lax.fori_loop(1, DEVICES, left_body, 0)
 
 
-def exchange(rows, cells, parts, factor):
+def exchange(rows, cells, parts, padded, gconv, table):
     dma = pltpu.SemaphoreType.DMA
     return pl.pallas_call(
-        functools.partial(exchange_kernel, factor),
+        exchange_kernel,
         out_shape=(
-            jax.ShapeDtypeStruct((LANES, 512), F32),
-            jax.ShapeDtypeStruct((512, LANES), F32),
-            jax.ShapeDtypeStruct((TAPS, TAPS, LANES), F32),
+            jax.ShapeDtypeStruct((LAT, PART_ROWS, LANES), BF16),
             jax.ShapeDtypeStruct((A_DEV, LANES), F32),
         ),
-        in_specs=[ANY_SPEC, ANY_SPEC, VMEM_SPEC],
-        out_specs=[VMEM_SPEC] * 4,
+        in_specs=[ANY_SPEC, ANY_SPEC, VMEM_SPEC, VMEM_SPEC, VMEM_SPEC, SMEM_SPEC],
+        out_specs=[VMEM_SPEC] * 2,
         scratch_shapes=[
+            pltpu.VMEM(padded.shape, F32),
+            pltpu.VMEM(gconv.shape, F32),
             pltpu.VMEM((DEVICES, LANES, LANES), BF16),
             pltpu.VMEM((DEVICES, 1, LANES), I32),
-            pltpu.VMEM((LAT, PART_ROWS, LANES), BF16),
+            pltpu.VMEM((LAT, LANES, LANES), BF16),
+            pltpu.VMEM((LAT, DW_ROWS, LANES), BF16),
+            pltpu.VMEM((LAT, DW_ROWS, LANES), BF16),
             pltpu.VMEM((LON, 16, LANES), BF16),
             pltpu.VMEM((LON, 16, LANES), BF16),
             pltpu.VMEM((8, LANES), F32),
@@ -555,12 +596,40 @@
             dma((DEVICES,)),
             dma((DEVICES,)),
             dma((DEVICES,)),
-            dma((4, LON)),
-            dma((4, LON)),
+            dma((5, LON)),
+            dma((5, LON)),
+            pltpu.SemaphoreType.REGULAR,
         ],
         compiler_params=pltpu.CompilerParams(collective_id=0, has_side_effects=True),
         name="exchange",
-    )(rows, cells.reshape(DEVICES, 1, LANES), parts)
+    )(rows, cells.reshape(DEVICES, 1, LANES), parts, padded, gconv, table)
+
+
+def finish_kernel(factor, chunks_ref, grad_ref, up_ref, down_ref, dw_ref, out_ref):
+    for chunk in range(LAT):
+        block = chunks_ref[chunk].astype(F32) * factor
+        if chunk < 4:
+            up_ref[:, chunk * LANES : (chunk + 1) * LANES] = block[:LANES]
+        else:
+            down_ref[(chunk - 4) * LANES : (chunk - 3) * LANES, :] = block[:LANES]
+        if chunk < TAPS:
+            dw_ref[chunk] = block[LANES : LANES + TAPS]
+    out_ref[...] = grad_ref[...]
+
+
+def finish(chunks, grad, factor):
+    return pl.pallas_call(
+        functools.partial(finish_kernel, factor),
+        out_shape=(
+            jax.ShapeDtypeStruct((LANES, 512), F32),
+            jax.ShapeDtypeStruct((512, LANES), F32),
+            jax.ShapeDtypeStruct((TAPS, TAPS, LANES), F32),
+            jax.ShapeDtypeStruct((A_DEV, LANES), F32),
+        ),
+        in_specs=[VMEM_SPEC] * 2,
+        out_specs=[VMEM_SPEC] * 4,
+        name="finish",
+    )(chunks, grad)
 
 
 def extended(block, sides, width, periodic):
@@ -598,7 +667,7 @@
     intersection_weights,
 ):
     rows, cols, channels = state.shape
-    slots, weights, cells = rank_entries(owner[:, 0], atmos_cell, weight_index, intersection_weights)
+    slots, cells = rank_entries(owner[:, 0], atmos_cell, weight_index)
 
     lon_ext = extended(state, (("lon", 1),), MARGIN, True)
     padded = extended(lon_ext, (("lat", 0),), MARGIN, False)
@@ -614,7 +683,7 @@
     chan = jnp.stack(
         [dw_bias, norm_gain, norm_bias, down_bias, layer_scale] + [jnp.zeros_like(dw_bias)] * 3
     )
-    result, parts, send_rows = run_block(
+    result, parts, send_rows, gconv = run_block(
         padded,
         state,
         forcing,
@@ -626,10 +695,10 @@
         up_bias.reshape(1, -1),
         down_weight,
         slots.reshape(-1),
-        weights.reshape(-1),
     )
     factor = float(rows * LAT * cols * LON) ** (-0.5)
-    grad_up, grad_down, grad_dw, forcing_grad = exchange(send_rows, cells, parts, factor)
+    chunks, grad = exchange(send_rows, cells, parts, padded, gconv, intersection_weights)
+    grad_up, grad_down, grad_dw, forcing_grad = finish(chunks, grad, factor)
     return (result, grad_dw, grad_up, grad_down, forcing_grad)
 
 

time: 167 us -> 137 us (0.82)
  the two profiles are of different devices: /device:TPU:65 before, /device:TPU:1 now
where the time goes in v2:
time: 137 us
  Pallas kernels  113 us (82%)
  starting transfers between devices  14.1 us (10%)
  local copies, waits for them, and re-layouts  3.05 us (2%)
  other arithmetic  2.64 us (2%)
  waiting for transfers between devices  2.62 us (2%)
    pallas_call x1, Pallas kernels, exchange(): pl.pallas_call(exchange_kernel, out_shape=(jax.ShapeDtypeStruct((LAT, PAR...  73.5 us
    pallas_call x1, Pallas kernels, run_block(): pl.pallas_call(block_kernel, out_shape=(jax.ShapeDtypeStruct(state.shape,...  32.8 us
    ppermute x2, starting transfers between devices, extended(): lax.ppermute(lax.slice_in_dim(block, block.shape[dim] - width, None, axis...  7.17 us
    pallas_call x1, Pallas kernels, rank_entries(): pl.pallas_call(rank_kernel, out_shape=(jax.ShapeDtypeStruct(shape, I32),...  5.02 us
    ppermute x1, starting transfers between devices, on_device(): lax.ppermute(lon_ext[rows - MARGIN:], 'lon', [(i, LON - 1 - i) for i in r...  4.24 us
  transfers between devices with their start and end apart: 5, of which 2 were waited for; matrix products, arithmetic and copies ran while one was open for 2% of the time, Pallas kernels for 4%

profile of v2, /device:TPU:1, one launch (start us, length us, event | category | flops | bytes accessed | tf_op | source)
XLA Modules:
  0.0 136.6 jit_solution(10563975554337724907)
XLA Ops:
  0.7 0.8 fusion.9
  1.5 1.5 %collective-permute-start.1 = (bf16[8,3,128]{2,1,0:T(4,128)(2,1)S(1)}, bf16[8,3,128]{2,1,0:T(4,128)(2,1)S(1)}, u32[]{:S(2)}, u32[]{:S(2)}) collective-permute-start(bf16[8,3,128]{2,1,0:T(4,128)(2,1)S(1)} %get-tuple-element.32), channel_id=1, source_target_pairs={{1,0},{2,1},{3,2},{4,3},{5,4},{6,5},{7,6},{8,7},{9,8},{10,9},{11,1... | collective-permute-start | bytes 18440 | tf_op jit(solution)/shard_map/ppermute | solution.py:645
  2.9 3.0 %collective-permute-start = (bf16[8,3,128]{2,1,0:T(4,128)(2,1)S(1)}, bf16[8,3,128]{2,1,0:T(4,128)(2,1)S(1)}, u32[]{:S(2)}, u32[]{:S(2)}) collective-permute-start(bf16[8,3,128]{2,1,0:T(4,128)(2,1)S(1)} %get-tuple-element.31), channel_id=1, source_target_pairs={{0,1},{1,2},{2,3},{3,4},{4,5},{5,6},{6,7},{7,8},{8,9},{9,10},{10,1... | collective-permute-start | bytes 18440 | tf_op jit(solution)/shard_map/ppermute | solution.py:642
  5.9 1.3 collective-permute-done.1
  7.2 1.4 collective-permute-done
  8.5 1.2 pad_maximum_fusion
  9.8 4.2 %collective-permute-start.3 = (bf16[3,390,128]{2,1,0:T(8,128)(2,1)S(1)}, bf16[3,390,128]{2,1,0:T(8,128)(2,1)S(1)}, u32[]{:S(2)}, u32[]{:S(2)}) collective-permute-start(bf16[3,390,128]{2,1,0:T(8,128)(2,1)S(1)} %get-tuple-element.30), channel_id=1, source_target_pairs={{0,15},{1,14},{2,13},{3,12},{4,11},{5,10},{6,9},{7,8},{8,7},{9,6},... | collective-permute-start | bytes 898568 | tf_op jit(solution)/shard_map/ppermute | solution.py:674
  14.0 1.3 collective-permute-start.4
  15.3 0.6 reshape.38.dw_ref
  15.9 0.0 copy-done.4
  15.9 0.0 copy-done.5
  16.0 0.6 stack.27.chan_ref
  16.6 4.2 %collective-permute-start.2 = (bf16[3,390,128]{2,1,0:T(8,128)(2,1)S(1)}, bf16[3,390,128]{2,1,0:T(8,128)(2,1)S(1)}, u32[]{:S(2)}, u32[]{:S(2)}) collective-permute-start(bf16[3,390,128]{2,1,0:T(8,128)(2,1)S(1)} %get-tuple-element.30), channel_id=1, source_target_pairs={{0,16},{16,32},{32,48},{48,64},{64,80},{80,96},{96,112},{1,17},{17... | collective-permute-start | bytes 898568 | tf_op jit(solution)/shard_map/ppermute | solution.py:642
  20.8 5.0 %rank_entries.1 = (s32[48,128]{1,0:T(8,128)}, s32[128,128]{1,0:T(8,128)}) custom-call(s32[48,128]{1,0:T(8,128)} %bitcast.17, s32[48,128]{1,0:T(8,128)} %bitcast.18, s32[48,128]{1,0:T(8,128)} %bitcast.19), custom_call_target="tpu_custom_call" | custom-call | flops 1000000000 | bytes 1000000 | tf_op jit(solution)/shard_map/rank_entries/pallas_call | solution.py:91
  25.8 0.0 collective-permute-done.3
  25.8 1.0 rev.3
  26.8 0.0 collective-permute-done.4
  26.8 0.1 broadcast_select_fusion
  26.9 0.0 collective-permute-done.2
  26.9 0.0 copy-done
  26.9 1.3 fusion.6.padded_ref
  28.2 32.8 %block_pass.1 = (bf16[8,384,128]{2,1,0:T(8,128)(2,1)}, bf16[8,128,128]{2,1,0:T(8,128)(2,1)}, bf16[128,96,128]{2,1,0:T(8,128)(2,1)}, bf16[8,384,128]{2,1,0:T(8,128)(2,1)}) custom-call(bf16[14,392,128]{2,1,0:T(8,128)(2,1)} %fusion.6.padded_ref, bf16[8,384,128]{2,1,0:T(8,128)(2,1)} %state_ref.1, bf16[8,384,128]{2,1,0:T(8,128)(2,1)} %forcing_ref.1, ...), custom_call_target="tpu_custom_call" | custom-call | flops 3000000000 | bytes 10000000 | tf_op jit(solution)/shard_map/block_pass/pallas_call | solution.py:258
  61.1 73.5 %exchange.1 = (bf16[8,144,128]{2,1,0:T(8,128)(2,1)}, f32[512,128]{1,0:T(8,128)}) custom-call(bf16[128,96,128]{2,1,0:T(8,128)(2,1)} %get-tuple-element.19.rows_hbm, s32[128,1,128]{2,1,0:T(1,128)} %bitcast.11, bf16[8,128,128]{2,1,0:T(8,128)(2,1)} %get-tuple-element.21.parts_ref, bf16[14,392,128]{2,1,0:T(8,128)(2,1)} %fusion.6.padded_ref, ...), custom_call_target="tpu_custom_call" | custom-call | tf_op jit(solution)/shard_map/exchange/pallas_call | solution.py:573
  134.6 2.0 %finish.1 = (f32[128,512]{1,0:T(8,128)}, f32[512,128]{1,0:T(8,128)}, f32[7,7,128]{2,1,0:T(8,128)}, f32[512,128]{1,0:T(8,128)}) custom-call(bf16[8,144,128]{2,1,0:T(8,128)(2,1)} %get-tuple-element.23.chunks_ref, f32[512,128]{1,0:T(8,128)} %get-tuple-element.24.grad_ref), custom_call_target="tpu_custom_call" | custom-call | tf_op jit(solution)/shard_map/finish/pallas_call | solution.py:621
  (13 shorter events, 0.0 us)
Async XLA Ops:
  0.6 14.7 %copy-start.1 = (bf16[7,7,128]{2,1,0:T(8,128)(2,1)S(1)}, bf16[7,7,128]{2,1,0:T(8,128)(2,1)}, u32[]{:S(2)}) copy-start(bf16[7,7,128]{2,1,0:T(8,128)(2,1)} %param.21) | copy-start | bytes 37636
  0.6 15.3 %copy-start.2 = (f32[128]{0:T(128)S(1)}, f32[128]{0:T(128)}, u32[]{:S(2)}) copy-start(f32[128]{0:T(128)} %param.22) | copy-start | bytes 1540
  0.7 15.3 %copy-start.3 = (f32[128]{0:T(128)S(1)}, f32[128]{0:T(128)}, u32[]{:S(2)}) copy-start(f32[128]{0:T(128)} %param.23) | copy-start | bytes 1540
  0.7 15.3 %copy-start.4 = (f32[128]{0:T(128)S(1)}, f32[128]{0:T(128)}, u32[]{:S(2)}) copy-start(f32[128]{0:T(128)} %param.24) | copy-start | bytes 1540
  0.7 15.3 %copy-start.5 = (f32[128]{0:T(128)S(1)}, f32[128]{0:T(128)}, u32[]{:S(2)}) copy-start(f32[128]{0:T(128)} %param.28) | copy-start | bytes 1540
  0.7 15.3 %copy-start.6 = (f32[128]{0:T(128)S(1)}, f32[128]{0:T(128)}, u32[]{:S(2)}) copy-start(f32[128]{0:T(128)} %param.29) | copy-start | bytes 1540
  1.5 5.7 %collective-permute-start.1 = (bf16[8,3,128]{2,1,0:T(4,128)(2,1)S(1)}, bf16[8,3,128]{2,1,0:T(4,128)(2,1)S(1)}, u32[]{:S(2)}, u32[]{:S(2)}) collective-permute-start(bf16[8,3,128]{2,1,0:T(4,128)(2,1)S(1)} %get-tuple-element.32), channel_id=1, source_target_pairs={{1,0},{2,1},{3,2},{4,3},{5,4},{6,5},{7,6},{8,7},{9,8},{10,9},{11,1... | collective-permute-start | bytes 18440 | tf_op jit(solution)/shard_map/ppermute | solution.py:645
  2.9 5.6 %collective-permute-start = (bf16[8,3,128]{2,1,0:T(4,128)(2,1)S(1)}, bf16[8,3,128]{2,1,0:T(4,128)(2,1)S(1)}, u32[]{:S(2)}, u32[]{:S(2)}) collective-permute-start(bf16[8,3,128]{2,1,0:T(4,128)(2,1)S(1)} %get-tuple-element.31), channel_id=1, source_target_pairs={{0,1},{1,2},{2,3},{3,4},{4,5},{5,6},{6,7},{7,8},{8,9},{9,10},{10,1... | collective-permute-start | bytes 18440 | tf_op jit(solution)/shard_map/ppermute | solution.py:642
  9.8 16.0 %collective-permute-start.3 = (bf16[3,390,128]{2,1,0:T(8,128)(2,1)S(1)}, bf16[3,390,128]{2,1,0:T(8,128)(2,1)S(1)}, u32[]{:S(2)}, u32[]{:S(2)}) collective-permute-start(bf16[3,390,128]{2,1,0:T(8,128)(2,1)S(1)} %get-tuple-element.30), channel_id=1, source_target_pairs={{0,15},{1,14},{2,13},{3,12},{4,11},{5,10},{6,9},{7,8},{8,7},{9,6},... | collective-permute-start | bytes 898568 | tf_op jit(solution)/shard_map/ppermute | solution.py:674
  14.0 12.8 %collective-permute-start.4 = (bf16[3,390,128]{2,1,0:T(8,128)(2,1)S(1)}, bf16[3,390,128]{2,1,0:T(8,128)(2,1)S(1)}, u32[]{:S(2)}, u32[]{:S(2)}) collective-permute-start(bf16[3,390,128]{2,1,0:T(8,128)(2,1)S(1)} %get-tuple-element.29), channel_id=1, source_target_pairs={{16,0},{32,16},{48,32},{64,48},{80,64},{96,80},{112,96},{17,1},{33... | collective-permute-start | bytes 898568 | tf_op jit(solution)/shard_map/ppermute | solution.py:645
  16.6 10.3 %collective-permute-start.2 = (bf16[3,390,128]{2,1,0:T(8,128)(2,1)S(1)}, bf16[3,390,128]{2,1,0:T(8,128)(2,1)S(1)}, u32[]{:S(2)}, u32[]{:S(2)}) collective-permute-start(bf16[3,390,128]{2,1,0:T(8,128)(2,1)S(1)} %get-tuple-element.30), channel_id=1, source_target_pairs={{0,16},{16,32},{32,48},{48,64},{64,80},{80,96},{96,112},{1,17},{17... | collective-permute-start | bytes 898568 | tf_op jit(solution)/shard_map/ppermute | solution.py:642
  25.8 1.1 copy-start

commit v3 on v2

--- a/solution.py
+++ b/solution.py
@@ -25,6 +25,8 @@
 DEVICES = LAT * LON
 PART_ROWS = 144
 STRIDE = 77
+EDGE = 16
+GROUP = 8
 DW_ROWS = 16
 CODE_BITS = 9
 
@@ -40,7 +42,7 @@
     return jnp.dot(a, b, preferred_element_type=F32)
 
 
-def rank_kernel(owner_ref, cell_ref, index_ref, slot_ref, cells_ref, base, acc):
+def rank_body(owner_ref, cell_ref, index_ref, slot_ref, cells_ref, base, acc):
     blocks = owner_ref.shape[0]
     group = 8
     base[...] = jnp.zeros_like(base)
@@ -85,21 +87,224 @@
     cells_ref[...] = (128.0 * total[:, :LANES] + total[:, LANES:]).astype(I32) - 1
 
 
-def rank_entries(owner, atmos_cell, weight_index):
+def halo_kernel(
+    state_ref,
+    owner_ref,
+    cell_ref,
+    index_ref,
+    pad_ref,
+    slot_ref,
+    cells_ref,
+    base,
+    acc,
+    from_left,
+    from_right,
+    from_up,
+    from_down,
+    up_left,
+    up_right,
+    down_left,
+    down_right,
+    send_sem,
+    recv_sem,
+):
+    lat = lax.axis_index("lat")
+    lon = lax.axis_index("lon")
+    rows, cols, channels = state_ref.shape
+    left = (lat, lax.rem(lon + LON - 1, LON))
+    right = (lat, lax.rem(lon + 1, LON))
+    above = (lat + 1, lon)
+    below = (lat - 1, lon)
+    fold = (lat, LON - 1 - lon)
+    top = rows - MARGIN
+    inner = lat < LAT - 1
+    folded = lat == LAT - 1
+    lower = lat > 0
+
+    barrier = pltpu.get_barrier_semaphore()
+
+    def greet(to):
+        pl.semaphore_signal(barrier, inc=1, device_id=to, device_id_type=MESH)
+
+    greet(left)
+    greet(right)
+
+    @pl.when(inner)
+    def _():
+        greet(above)
+
+    @pl.when(folded)
+    def _():
+        greet(fold)
+
+    @pl.when(lower)
+    def _():
+        greet(below)
+        pl.semaphore_wait(barrier, 4)
+
+    @pl.when(lat == 0)
+    def _():
+        pl.semaphore_wait(barrier, 3)
+
+    def copy(number, src, dst, to):
+        return pltpu.make_async_remote_copy(
+            src_ref=src,
+            dst_ref=dst[0],
+            send_sem=send_sem.at[number],
+            recv_sem=recv_sem.at[dst[1]],
+            device_id=to,
+            device_id_type=MESH,
+        )
+
+    bottom_rows = state_ref.at[pl.ds(0, MARGIN)]
+    top_rows = state_ref.at[pl.ds(top, MARGIN)]
+    to_left = copy(0, state_ref.at[:, pl.ds(0, EDGE)], (from_right, 0), left)
+    to_right = copy(1, state_ref.at[:, pl.ds(cols - EDGE, EDGE)], (from_left, 1), right)
+    down_main = copy(2, bottom_rows, (from_up, 2), below)
+    up_main = copy(3, top_rows, (from_down, 3), above)
+    fold_main = copy(3, top_rows, (from_up, 2), fold)
+    down_l = copy(4, from_left.at[pl.ds(0, MARGIN)], (up_left, 4), below)
+    down_r = copy(5, from_right.at[pl.ds(0, MARGIN)], (up_right, 5), below)
+    up_l = copy(6, from_left.at[pl.ds(top, MARGIN)], (down_left, 6), above)
+    up_r = copy(7, from_right.at[pl.ds(top, MARGIN)], (down_right, 7), above)
+    fold_l = copy(6, from_left.at[pl.ds(top, MARGIN)], (up_right, 5), fold)
+    fold_r = copy(7, from_right.at[pl.ds(top, MARGIN)], (up_left, 4), fold)
+
+    to_left.start()
+    to_right.start()
+
+    @pl.when(lower)
+    def _():
+        down_main.start()
+
+    @pl.when(inner)
+    def _():
+        up_main.start()
+
+    @pl.when(folded)
+    def _():
+        fold_main.start()
+
+    to_left.wait_recv()
+    to_right.wait_recv()
+
+    @pl.when(lower)
+    def _():
+        down_l.start()
+        down_r.start()
+
+    @pl.when(inner)
+    def _():
+        up_l.start()
+        up_r.start()
+
+    @pl.when(folded)
+    def _():
+        fold_l.start()
+        fold_r.start()
+
+    right_at = MARGIN + cols
+
+    def place(line, main, on_left, on_right):
+        pad_ref[line, MARGIN:right_at, :] = main.astype(F32)
+        pad_ref[line, 0:MARGIN, :] = on_left.astype(F32)[EDGE - MARGIN :]
+        pad_ref[line, right_at : right_at + MARGIN, :] = on_right.astype(F32)[:MARGIN]
+
+    pad_ref[:, right_at + MARGIN :, :] = jnp.zeros(
+        (rows + 2 * MARGIN, pad_ref.shape[1] - right_at - MARGIN, channels), F32
+    )
+    for r in range(rows):
+        place(MARGIN + r, state_ref[r], from_left[r], from_right[r])
+
+    rank_body(owner_ref, cell_ref, index_ref, slot_ref, cells_ref, base, acc)
+
+    down_main.wait_recv()
+    down_l.wait_recv()
+    down_r.wait_recv()
+
+    @pl.when(inner)
+    def _():
+        for m in range(MARGIN):
+            place(MARGIN + rows + m, from_up[m], up_left[m], up_right[m])
+
+    @pl.when(folded)
+    def _():
+        def flip(size):
+            ids = [lax.broadcasted_iota(I32, (size, size), d) for d in range(2)]
+            return jnp.where(ids[0] + ids[1] == size - 1, 1.0, 0.0).astype(BF16)
+
+        swap = flip(LANES)
+        swap_edge = flip(EDGE)
+        for m in range(MARGIN):
+            line = MARGIN + rows + m
+            source = MARGIN - 1 - m
+            for q in range(cols // LANES):
+                first = cols - (q + 1) * LANES
+                pad_ref[line, MARGIN + q * LANES : MARGIN + (q + 1) * LANES, :] = nn_dot(
+                    swap, from_up[source, first : first + LANES, :]
+                )
+            pad_ref[line, 0:MARGIN, :] = nn_dot(swap_edge, up_left[source])[EDGE - MARGIN :]
+            pad_ref[line, right_at : right_at + MARGIN, :] = nn_dot(swap_edge, up_right[source])[:MARGIN]
+
+    @pl.when(lower)
+    def _():
+        up_main.wait_recv()
+        up_l.wait_recv()
+        up_r.wait_recv()
+        for m in range(MARGIN):
+            place(m, from_down[m], down_left[m], down_right[m])
+
+    @pl.when(lat == 0)
+    def _():
+        pad_ref[0:MARGIN] = jnp.zeros((MARGIN,) + pad_ref.shape[1:], F32)
+
+    to_left.wait_send()
+    to_right.wait_send()
+    up_main.wait_send()
+    up_l.wait_send()
+    up_r.wait_send()
+
+    @pl.when(lower)
+    def _():
+        down_main.wait_send()
+        down_l.wait_send()
+        down_r.wait_send()
+
+
+def exchange_halo(state, owner, atmos_cell, weight_index):
+    rows, cols, channels = state.shape
     entries = owner.shape[0]
     shape = (entries // LANES, LANES)
+    dma = pltpu.SemaphoreType.DMA
+    edge = pltpu.VMEM((rows, EDGE, channels), BF16)
+    strip = pltpu.VMEM((MARGIN, cols, channels), BF16)
+    corner = pltpu.VMEM((MARGIN, EDGE, channels), BF16)
     return pl.pallas_call(
-        rank_kernel,
+        halo_kernel,
         out_shape=(
+            jax.ShapeDtypeStruct((rows + 2 * MARGIN, cols + 8, channels), F32),
             jax.ShapeDtypeStruct(shape, I32),
             jax.ShapeDtypeStruct((DEVICES, LANES), I32),
         ),
-        in_specs=[VMEM_SPEC, VMEM_SPEC, VMEM_SPEC],
-        out_specs=[VMEM_SPEC, VMEM_SPEC],
-        scratch_shapes=[pltpu.VMEM((LANES, LANES), F32), pltpu.VMEM((LANES, 2 * LANES), F32)],
-        name="rank_entries",
-        cost_estimate=pl.CostEstimate(flops=10**9, bytes_accessed=10**6, transcendentals=0),
-    )(owner.reshape(shape), atmos_cell.reshape(shape), weight_index.reshape(shape))
+        in_specs=[VMEM_SPEC] * 4,
+        out_specs=[VMEM_SPEC] * 3,
+        scratch_shapes=[
+            pltpu.VMEM((LANES, LANES), F32),
+            pltpu.VMEM((LANES, 2 * LANES), F32),
+            edge,
+            edge,
+            strip,
+            strip,
+            corner,
+            corner,
+            corner,
+            corner,
+            dma((8,)),
+            dma((8,)),
+        ],
+        compiler_params=pltpu.CompilerParams(collective_id=1, has_side_effects=True),
+        name="exchange_halo",
+    )(state, owner.reshape(shape), atmos_cell.reshape(shape), weight_index.reshape(shape))
 
 
 def block_kernel(
@@ -109,7 +314,11 @@
     cot_ref,
     land_ref,
     dw_ref,
-    chan_ref,
+    dw_bias_ref,
+    gain_ref,
+    shift_ref,
+    down_bias_ref,
+    scale_ref,
     up_ref,
     up_bias_ref,
     down_ref,
@@ -118,7 +327,6 @@
     parts_ref,
     send_ref,
     gconv_ref,
-    xf,
     wts,
     conv,
     gm,
@@ -133,11 +341,11 @@
 ):
     rows, cols, channels = state_ref.shape
     hidden_units = up_ref.shape[1]
-    dw_bias = chan_ref[0:1, :]
-    gain = chan_ref[1:2, :]
-    shift = chan_ref[2:3, :]
-    down_bias = chan_ref[3:4, :]
-    scale = chan_ref[4:5, :]
+    dw_bias = dw_bias_ref[...]
+    gain = gain_ref[...]
+    shift = shift_ref[...]
+    down_bias = down_bias_ref[...]
+    scale = scale_ref[...]
 
     def zero_body(i, carry):
         buf[pl.ds(pl.multiple_of(i * 128, 128), 128), :] = jnp.zeros((128, channels), F32)
@@ -147,19 +355,16 @@
     up_acc[...] = jnp.zeros_like(up_acc)
     down_acc[...] = jnp.zeros_like(down_acc)
 
-    def unpack(i, carry):
-        xf[i] = padded_ref[i].astype(F32)
-        return carry
-
-    lax.fori_loop(0, rows + 2 * MARGIN, unpack, 0)
-    for tap in range(TAPS * TAPS):
-        wts[tap] = jnp.broadcast_to(dw_ref[tap : tap + 1, :], (8, channels))
+    for a in range(TAPS):
+        taps = dw_ref[a].astype(F32)
+        for b in range(TAPS):
+            wts[a * TAPS + b] = jnp.broadcast_to(taps[b : b + 1, :], (8, channels))
 
     def conv_body(block, carry):
         start = block * 8
         total = [jnp.broadcast_to(dw_bias, (8, channels)) for _ in range(rows)]
         for b in range(TAPS):
-            xs = [xf[line, pl.ds(start + b, 8), :] for line in range(rows + TAPS - 1)]
+            xs = [padded_ref[line, pl.ds(start + b, 8), :] for line in range(rows + TAPS - 1)]
             for a in range(TAPS):
                 wv = wts[a * TAPS + b]
                 for r in range(rows):
@@ -250,11 +455,9 @@
     lax.fori_loop(0, DEVICES // group, cast_body, 0)
 
 
-def run_block(padded, state, forcing, cotangent, land, dw, chan, up, up_bias, down, slots):
+def run_block(padded, state, forcing, cotangent, land, dw, vectors, up, up_bias, down, slots):
     rows, cols, channels = state.shape
     hidden = up.shape[1]
-    wide = padded.shape[1]
-    lines = padded.shape[0]
     return pl.pallas_call(
         block_kernel,
         out_shape=(
@@ -263,10 +466,9 @@
             jax.ShapeDtypeStruct((DEVICES, CAP, channels), BF16),
             jax.ShapeDtypeStruct(state.shape, BF16),
         ),
-        in_specs=[VMEM_SPEC] * 10 + [SMEM_SPEC],
+        in_specs=[VMEM_SPEC] * 14 + [SMEM_SPEC],
         out_specs=[VMEM_SPEC] * 4,
         scratch_shapes=[
-            pltpu.VMEM((lines, wide, channels), F32),
             pltpu.VMEM((TAPS * TAPS, 8, channels), F32),
             pltpu.VMEM((rows, cols, channels), F32),
             pltpu.VMEM((rows * cols, channels), F32),
@@ -283,7 +485,7 @@
         cost_estimate=pl.CostEstimate(
             flops=3 * 10**9, bytes_accessed=10**7, transcendentals=rows * cols * hidden
         ),
-    )(padded, state, forcing, cotangent, land, dw, chan, up, up_bias, down, slots)
+    )(padded, state, forcing, cotangent, land, dw, *vectors, up, up_bias, down, slots)
 
 
 def exchange_kernel(
@@ -295,7 +497,6 @@
     table_ref,
     chunks_ref,
     grad_ref,
-    xf,
     gf,
     recv_rows,
     recv_cells,
@@ -312,6 +513,7 @@
     row_recv,
     cell_send,
     cell_recv,
+    own_sem,
     send_sem,
     recv_sem,
     entered,
@@ -344,52 +546,55 @@
     lax.fori_loop(1, LON, greet_lon, 0)
     lax.fori_loop(1, LAT, greet_lat, 0)
 
-    recv_rows[:, CAP:, :] = jnp.zeros((DEVICES, LANES - CAP, LANES), BF16)
-    grad_ref[...] = jnp.zeros_like(grad_ref)
-    pl.semaphore_wait(barrier, LON + LAT - 2)
-    lax.fori_loop(1, LAT, pass_on, 0)
-    pl.semaphore_wait(entered, LAT - 1)
-
     def row_copy(k):
         to = device(k)
-        peer = to[0] * LON + to[1]
-        return (
-            pltpu.make_async_remote_copy(
-                src_ref=rows_hbm.at[peer],
-                dst_ref=recv_rows.at[k, pl.ds(0, CAP)],
-                send_sem=row_send.at[k],
-                recv_sem=row_recv.at[k],
-                device_id=to,
-                device_id_type=MESH,
-            ),
-            pltpu.make_async_remote_copy(
-                src_ref=cells_hbm.at[peer],
-                dst_ref=recv_cells.at[k],
-                send_sem=cell_send.at[k],
-                recv_sem=cell_recv.at[k],
-                device_id=to,
-                device_id_type=MESH,
-            ),
+        return pltpu.make_async_remote_copy(
+            src_ref=rows_hbm.at[to[0] * LON + to[1]],
+            dst_ref=recv_rows.at[k, pl.ds(0, CAP)],
+            send_sem=row_send.at[0],
+            recv_sem=row_recv.at[k // GROUP],
+            device_id=to,
+            device_id_type=MESH,
+        )
+
+    def cell_copy(k):
+        to = device(k)
+        return pltpu.make_async_remote_copy(
+            src_ref=cells_hbm.at[to[0] * LON + to[1]],
+            dst_ref=recv_cells.at[k],
+            send_sem=cell_send.at[0],
+            recv_sem=cell_recv.at[0],
+            device_id=to,
+            device_id_type=MESH,
         )
 
     def send_range(first, last):
         def body(k, carry):
-            for copy in row_copy(k):
-                copy.start()
+            row_copy(k).start()
             return carry
 
         lax.fori_loop(first, last, body, 0)
 
-    own_rows = pltpu.make_async_copy(rows_hbm.at[me], recv_rows.at[0, pl.ds(0, CAP)], row_recv.at[0])
-    own_cells = pltpu.make_async_copy(cells_hbm.at[me], recv_cells.at[0], cell_recv.at[0])
+    def send_cells():
+        def body(k, carry):
+            cell_copy(k).start()
+            return carry
+
+        lax.fori_loop(1, DEVICES, body, 0)
+
+    def await_bytes(ref, sem):
+        pltpu.make_async_copy(ref, ref, sem).wait()
+
+    own_rows = pltpu.make_async_copy(rows_hbm.at[me], recv_rows.at[0, pl.ds(0, CAP)], own_sem.at[0])
+    own_cells = pltpu.make_async_copy(cells_hbm.at[me], recv_cells.at[0], own_sem.at[1])
 
     def lat_copy(stage, k, src, dst):
         to = lax.rem(lat + k, LAT)
         return pltpu.make_async_remote_copy(
             src_ref=src(to),
             dst_ref=dst.at[k],
-            send_sem=send_sem.at[stage, k],
-            recv_sem=recv_sem.at[stage, k],
+            send_sem=send_sem.at[stage],
+            recv_sem=recv_sem.at[stage],
             device_id=(to, lon),
             device_id_type=MESH,
         )
@@ -399,8 +604,8 @@
         return pltpu.make_async_remote_copy(
             src_ref=src(to),
             dst_ref=dst.at[k],
-            send_sem=send_sem.at[stage, k],
-            recv_sem=recv_sem.at[stage, k],
+            send_sem=send_sem.at[stage],
+            recv_sem=recv_sem.at[stage],
             device_id=(lat, to),
             device_id_type=MESH,
         )
@@ -427,44 +632,34 @@
 
         lax.fori_loop(1, count, body, 0)
 
-    def arrive_all(copy, count):
-        def body(k, carry):
-            copy(k).wait_recv()
-            return carry
-
-        lax.fori_loop(1, count, body, 0)
-
-    def left_all(copy, count):
-        def body(k, carry):
-            copy(k).wait_send()
-            return carry
-
-        lax.fori_loop(1, count, body, 0)
-
-    start_all(copy1, LAT)
+    def arrive_all(stage, dst):
+        await_bytes(dst.at[pl.ds(1, dst.shape[0] - 1)], recv_sem.at[stage])
+
+    def left_all(stage, dst):
+        await_bytes(dst.at[pl.ds(1, dst.shape[0] - 1)], send_sem.at[stage])
+
     own_rows.start()
     own_cells.start()
-    send_range(1, 40)
-
-    lines, wide, channels = xf.shape
+    recv_rows[:, CAP:, :] = jnp.zeros((DEVICES, LANES - CAP, LANES), BF16)
+    grad_ref[...] = jnp.zeros_like(grad_ref)
+
+    lines, wide, channels = padded_ref.shape
     out_lines, cols = gf.shape[0], gf.shape[1]
-
-    def unpack_x(i, carry):
-        xf[i] = padded_ref[i].astype(F32)
-        return carry
 
     def unpack_g(i, carry):
         gf[i] = gconv_ref[i].astype(F32)
         return carry
 
-    lax.fori_loop(0, lines, unpack_x, 0)
     lax.fori_loop(0, out_lines, unpack_g, 0)
     sums = [[None] * TAPS for _ in range(TAPS)]
     for b in range(TAPS):
+        if b == 4:
+            pl.semaphore_wait(barrier, LON + LAT - 2)
+            lax.fori_loop(1, LAT, pass_on, 0)
 
         def corr_body(block, carry):
             start = block * 8
-            xs = [xf[line, pl.ds(start + b, 8), :] for line in range(lines)]
+            xs = [padded_ref[line, pl.ds(start + b, 8), :] for line in range(lines)]
             gs = [gf[r, pl.ds(pl.multiple_of(start, 8), 8), :] for r in range(out_lines)]
             out = []
             for a in range(TAPS):
@@ -484,10 +679,14 @@
         dw_part[a] = jnp.concatenate(lines_a, axis=0).astype(BF16)
     dw_part[TAPS] = jnp.zeros((DW_ROWS, channels), BF16)
 
+    pl.semaphore_wait(entered, LAT - 1)
+
+    start_all(copy1, LAT)
     start_all(copy_dw, LAT)
-    send_range(40, 64)
-    arrive_all(copy1, LAT)
-    arrive_all(copy_dw, LAT)
+    send_cells()
+    send_range(1, 24)
+    arrive_all(0, recv1)
+    arrive_all(4, recv_dw)
     total = parts_ref[lat].astype(F32)
     tail = dw_part[lat].astype(F32)
     for k in range(1, LAT):
@@ -498,8 +697,8 @@
         send2[j] = jnp.concatenate([total[8 * j : 8 * j + 8, :], tail], axis=0).astype(BF16)
 
     start_all(copy2, LON)
-    send_range(64, 88)
-    arrive_all(copy2, LON)
+    send_range(24, 48)
+    arrive_all(1, recv2)
     total = send2[lon].astype(F32)
     for k in range(1, LON):
         total = total + recv2[k].astype(F32)
@@ -507,14 +706,15 @@
     send4[LANES:, :] = jnp.concatenate([total[8:, :], jnp.zeros((8, LANES), F32)], axis=0).astype(BF16)
 
     start_all(copy3, LON)
-    send_range(88, DEVICES)
-    arrive_all(copy3, LON)
+    send_range(48, 72)
+    arrive_all(2, recv3)
     recv3[0] = send3[...]
     for j in range(LON // 2):
         pair = [recv3[lax.rem(lon - (2 * j + i) + LON, LON)] for i in range(2)]
         send4[16 * j : 16 * j + 16, :] = jnp.concatenate(pair, axis=0).astype(BF16)
 
     start_all(copy4, LAT)
+    send_range(72, DEVICES)
 
     cell_id = lax.broadcasted_iota(I32, (A_DEV, LANES), 0)
 
@@ -532,40 +732,34 @@
         values = recv_rows[pl.ds(2 * i, 2)].reshape(2 * LANES, LANES)
         grad_ref[...] += nn_dot(hot, values)
 
-    def wait_rows(k):
-        for copy in row_copy(k):
-            copy.wait_recv()
-
     own_rows.wait()
     own_cells.wait()
-    wait_rows(1)
-    add_pair(0)
-
-    def pair_body(i, carry):
-        wait_rows(2 * i)
-        wait_rows(2 * i + 1)
+    await_bytes(recv_cells.at[pl.ds(1, DEVICES - 1)], cell_recv.at[0])
+    await_bytes(recv_rows.at[pl.ds(1, GROUP - 1), pl.ds(0, CAP)], row_recv.at[0])
+    for i in range(GROUP // 2):
         add_pair(i)
-        return carry
-
-    lax.fori_loop(1, DEVICES // 2, pair_body, 0)
-
-    arrive_all(copy4, LAT)
+
+    def group_body(g, carry):
+        await_bytes(recv_rows.at[pl.ds(g * GROUP, GROUP), pl.ds(0, CAP)], row_recv.at[g])
+        for i in range(GROUP // 2):
+            add_pair(g * (GROUP // 2) + i)
+        return carry
+
+    lax.fori_loop(1, DEVICES // GROUP, group_body, 0)
+
+    arrive_all(3, recv4)
     recv4[0] = send4[...]
     for chunk in range(LAT):
         chunks_ref[chunk] = recv4[lax.rem(lat - chunk + LAT, LAT)]
 
-    left_all(copy1, LAT)
-    left_all(copy_dw, LAT)
-    left_all(copy2, LON)
-    left_all(copy3, LON)
-    left_all(copy4, LAT)
-
-    def left_body(k, carry):
-        for copy in row_copy(k):
-            copy.wait_send()
-        return carry
-
-    lax.fori_loop(1, DEVICES, left_body, 0)
+    left_all(0, recv1)
+    left_all(4, recv_dw)
+    left_all(1, recv2)
+    left_all(2, recv3)
+    left_all(3, recv4)
+
+    await_bytes(recv_rows.at[pl.ds(1, DEVICES - 1), pl.ds(0, CAP)], row_send.at[0])
+    await_bytes(recv_cells.at[pl.ds(1, DEVICES - 1)], cell_send.at[0])
 
 
 def exchange(rows, cells, parts, padded, gconv, table):
@@ -579,7 +773,6 @@
         in_specs=[ANY_SPEC, ANY_SPEC, VMEM_SPEC, VMEM_SPEC, VMEM_SPEC, SMEM_SPEC],
         out_specs=[VMEM_SPEC] * 2,
         scratch_shapes=[
-            pltpu.VMEM(padded.shape, F32),
             pltpu.VMEM(gconv.shape, F32),
             pltpu.VMEM((DEVICES, LANES, LANES), BF16),
             pltpu.VMEM((DEVICES, 1, LANES), I32),
@@ -592,12 +785,13 @@
             pltpu.VMEM((LON, 8, LANES), F32),
             pltpu.VMEM((PART_ROWS, LANES), BF16),
             pltpu.VMEM((LAT, PART_ROWS, LANES), BF16),
-            dma((DEVICES,)),
-            dma((DEVICES,)),
-            dma((DEVICES,)),
-            dma((DEVICES,)),
-            dma((5, LON)),
-            dma((5, LON)),
+            dma((1,)),
+            dma((DEVICES // GROUP,)),
+            dma((1,)),
+            dma((1,)),
+            dma((2,)),
+            dma((5,)),
+            dma((5,)),
             pltpu.SemaphoreType.REGULAR,
         ],
         compiler_params=pltpu.CompilerParams(collective_id=0, has_side_effects=True),
@@ -630,21 +824,6 @@
         out_specs=[VMEM_SPEC] * 4,
         name="finish",
     )(chunks, grad)
-
-
-def extended(block, sides, width, periodic):
-    for axis, dim in sides:
-        count = lax.axis_size(axis)
-        forward = [(i, i + 1) for i in range(count - 1)]
-        if periodic:
-            forward.append((count - 1, 0))
-        backward = [(target, source) for source, target in forward]
-        low = lax.ppermute(
-            lax.slice_in_dim(block, block.shape[dim] - width, None, axis=dim), axis, forward
-        )
-        high = lax.ppermute(lax.slice_in_dim(block, 0, width, axis=dim), axis, backward)
-        block = jnp.concatenate([low, block, high], axis=dim)
-    return block
 
 
 def on_device(
@@ -667,30 +846,19 @@
     intersection_weights,
 ):
     rows, cols, channels = state.shape
-    slots, cells = rank_entries(owner[:, 0], atmos_cell, weight_index)
-
-    lon_ext = extended(state, (("lon", 1),), MARGIN, True)
-    padded = extended(lon_ext, (("lat", 0),), MARGIN, False)
-    partner = lax.ppermute(
-        lon_ext[rows - MARGIN :], "lon", [(i, LON - 1 - i) for i in range(LON)]
-    )
-    mirrored = partner[::-1, ::-1]
-    northmost = lax.axis_index("lat") == LAT - 1
-    north_rows = jnp.where(northmost, mirrored, padded[rows + MARGIN :])
-    padded = jnp.concatenate([padded[: rows + MARGIN], north_rows], axis=0)
-    padded = jnp.pad(padded, ((0, 0), (0, 2), (0, 0)))
-
-    chan = jnp.stack(
-        [dw_bias, norm_gain, norm_bias, down_bias, layer_scale] + [jnp.zeros_like(dw_bias)] * 3
-    )
+    padded, slots, cells = exchange_halo(state, owner[:, 0], atmos_cell, weight_index)
+    vectors = [
+        array.reshape(1, channels)
+        for array in (dw_bias, norm_gain, norm_bias, down_bias, layer_scale)
+    ]
     result, parts, send_rows, gconv = run_block(
         padded,
         state,
         forcing,
         cotangent,
         land_mask,
-        dw_weight.astype(F32).reshape(TAPS * TAPS, channels),
-        chan,
+        dw_weight,
+        vectors,
         up_weight,
         up_bias.reshape(1, -1),
         down_weight,

time: 137 us -> 122 us (0.89)
  starting transfers between devices: 14.1 us -> 0 us
  Pallas kernels: 113 us -> 121 us
  local copies, waits for them, and re-layouts: 3.05 us -> 0 us
  other arithmetic: 2.64 us -> 0 us
  waiting for transfers between devices: 2.62 us -> 0 us
    ppermute x5 -> x0, starting transfers between devices: 14.1 us -> none  [the longest x2 7.17 us: extended(): lax.ppermute(lax.slice_in_dim(block, block.shape[dim] - width, None, axis...]
    pallas_call x1, Pallas kernels: 5.02 us -> 14.9 us  [exchange_halo(): pl.pallas_call(halo_kernel, out_shape=(jax.ShapeDtypeStruct((rows + 2 * M...]
    ppermute x5 -> x0, waiting for transfers between devices: 2.62 us -> none  [the longest x2 1.36 us: extended(): lax.ppermute(lax.slice_in_dim(block, block.shape[dim] - width, None, axis...]
    concatenate x2 -> x0, other arithmetic: 2.56 us -> none  [the longest x1 1.34 us: on_device(): padded = jnp.concatenate([padded[:rows + MARGIN], north_rows], axis=0)]
    pallas_call x1, Pallas kernels: 73.5 us -> 71.4 us  [exchange(): pl.pallas_call(exchange_kernel, out_shape=(jax.ShapeDtypeStruct((LAT, PAR...]
  transfers between devices with their start and end apart: 5 -> 0, of which waited for: 2 -> 0; matrix products, arithmetic and copies ran while one was open for 2% -> 0% of each run, Pallas kernels for 4% -> 0%
where the time goes in v3:
time: 122 us
  Pallas kernels  121 us (99%)
    pallas_call x1, Pallas kernels, exchange(): pl.pallas_call(exchange_kernel, out_shape=(jax.ShapeDtypeStruct((LAT, PAR...  71.4 us
    pallas_call x1, Pallas kernels, run_block(): pl.pallas_call(block_kernel, out_shape=(jax.ShapeDtypeStruct(state.shape,...  33 us
    pallas_call x1, Pallas kernels, exchange_halo(): pl.pallas_call(halo_kernel, out_shape=(jax.ShapeDtypeStruct((rows + 2 * M...  14.9 us

profile of v3, /device:TPU:1, one launch (start us, length us, event | category | flops | bytes accessed | tf_op | source)
XLA Modules:
  0.0 121.9 jit_solution(11586122081104472655)
XLA Ops:
  0.6 14.9 %exchange_halo.1 = (f32[14,392,128]{2,1,0:T(8,128)}, s32[48,128]{1,0:T(8,128)}, s32[128,128]{1,0:T(8,128)}) custom-call(bf16[8,384,128]{2,1,0:T(8,128)(2,1)} %state_ref.3, s32[48,128]{1,0:T(8,128)} %bitcast.12, s32[48,128]{1,0:T(8,128)} %bitcast.13, s32[48,128]{1,0:T(8,128)} %bitcast.14), custom_call_target="tpu_custom_call" | custom-call | tf_op jit(solution)/shard_map/exchange_halo/pallas_call | solution.py:282
  15.5 33.0 %block_pass.1 = (bf16[8,384,128]{2,1,0:T(8,128)(2,1)}, bf16[8,128,128]{2,1,0:T(8,128)(2,1)}, bf16[128,96,128]{2,1,0:T(8,128)(2,1)}, bf16[8,384,128]{2,1,0:T(8,128)(2,1)}) custom-call(f32[14,392,128]{2,1,0:T(8,128)} %get-tuple-element.18.padded_ref, bf16[8,384,128]{2,1,0:T(8,128)(2,1)} %state_ref.3, bf16[8,384,128]{2,1,0:T(8,128)(2,1)} %forcing_ref.1, ...), custom_call_target="tpu_custom_call" | custom-call | flops 3000000000 | bytes 10000000 | tf_op jit(solution)/shard_map/block_pass/pallas_call | solution.py:461
  48.5 71.4 %exchange.1 = (bf16[8,144,128]{2,1,0:T(8,128)(2,1)}, f32[512,128]{1,0:T(8,128)}) custom-call(bf16[128,96,128]{2,1,0:T(8,128)(2,1)} %get-tuple-element.21.rows_hbm, s32[128,1,128]{2,1,0:T(1,128)} %bitcast.11, bf16[8,128,128]{2,1,0:T(8,128)(2,1)} %get-tuple-element.23.parts_ref, f32[14,392,128]{2,1,0:T(8,128)} %get-tuple-element.18.padded_ref, ...), custom_call_target="tpu_custom_call" | custom-call | tf_op jit(solution)/shard_map/exchange/pallas_call | solution.py:767
  119.9 2.0 %finish.1 = (f32[128,512]{1,0:T(8,128)}, f32[512,128]{1,0:T(8,128)}, f32[7,7,128]{2,1,0:T(8,128)}, f32[512,128]{1,0:T(8,128)}) custom-call(bf16[8,144,128]{2,1,0:T(8,128)(2,1)} %get-tuple-element.25.chunks_ref, f32[512,128]{1,0:T(8,128)} %get-tuple-element.26.grad_ref), custom_call_target="tpu_custom_call" | custom-call | tf_op jit(solution)/shard_map/finish/pallas_call | solution.py:815
